TPU v7x, 256 devices: a whole 4x4x8 slice. The times are simulated.
256 devices in a mesh: row: 16 (over y, z_hi, core), col: 16 (over x, z_lo).
Axes of the slice: x: 4, y: 4, z: 8 (z_hi: 2, z_lo: 4; z = z_hi * 4 + z_lo), core: 2. Of those that a mesh axis runs over, the one named last changes fastest.
Arguments:
- eigvec: float32 [16384, 20480], P('row', 'col'), may hold values from -6 to 6
- panels: float32 [3, 16384, 256], P(None, ('row', 'col')), may hold values from -0.375 to 0.375
- factors: float32 [3, 256, 256], replicated, may hold values from -0.046875 to 0.046875
Outputs:
- updated: float32 [16384, 20480], P('row', 'col')
All inputs are finite; a program needn't handle non-finite values.
Results may differ from a plain program's by a relative error of at most 0.00012.
Values sent between devices are 32-bit elements; how exact they have to be, the bound alone decides.
No kernel may reach another device: no remote copies, remote signals or barrier semaphores. Data moves between devices by JAX's collectives and lax.ppermute only.
A program may use at most 64 MiB of HBM per device.

v0:
```python
import functools

import jax
import jax.numpy as jnp
import numpy as np
from jax import lax
from jax.experimental import pallas as pl
from jax.experimental.pallas import tpu as pltpu
from jax.sharding import PartitionSpec as P


NREF = 3
BF = jnp.bfloat16
F32 = jnp.float32


def lin(y, zh, c, x, zl):
    return ((y * 2 + zh) * 2 + c) * 16 + x * 4 + zl


def xor_pair(core):
    return (1, 3) if core == 0 else (3, 1)


def perm_of(f):
    pairs = []
    for y in range(4):
        for zh in range(2):
            for c in range(2):
                for x in range(4):
                    for zl in range(4):
                        pairs.append((lin(y, zh, c, x, zl), lin(*f(y, zh, c, x, zl))))
    return pairs


CORE = perm_of(lambda y, zh, c, x, zl: (y, zh, 1 - c, x, zl))
Y1 = perm_of(lambda y, zh, c, x, zl: (y ^ xor_pair(c)[0], zh, c, x, zl))
Y2 = perm_of(lambda y, zh, c, x, zl: (y ^ xor_pair(c)[1], zh, c, x, zl))
X1 = perm_of(lambda y, zh, c, x, zl: (y, zh, c, x ^ xor_pair(c)[0], zl))
X2 = perm_of(lambda y, zh, c, x, zl: (y, zh, c, x ^ xor_pair(c)[1], zl))
ZH = perm_of(lambda y, zh, c, x, zl: (y, 1 - zh, c, x, zl))
ZL = [perm_of(lambda y, zh, c, x, zl, d=d: (y, zh, c, x, zl ^ d)) for d in range(4)]


def send(a, perm):
    return lax.ppermute(a, ("row", "col"), perm)


def tables():
    piece = np.zeros((16, 8), np.int32)
    block = np.zeros((2, 16, 16), np.int32)
    for r in range(16):
        y, c = r // 4, r % 2
        for p in range(8):
            b0, b1, b2 = p // 4, (p // 2) % 2, p % 2
            owner = c ^ b0
            g = xor_pair(owner)
            piece[r, p] = owner * 4 + (y ^ (b1 * g[0]) ^ (b2 * g[1]))
    for c in range(2):
        g = xor_pair(c)
        for j in range(16):
            x, zl = j // 4, j % 4
            for p in range(16):
                b2, b1, zp = p // 8, (p // 4) % 2, p % 4
                block[c, j, p] = (x ^ (b1 * g[0]) ^ (b2 * g[1])) * 4 + (zl ^ zp)
    return piece, block


def split(v):
    hi = v.astype(BF)
    return hi, (v - hi.astype(F32)).astype(BF)


def dot3(ah, al, bh, bl, dims=(((1,), (0,)), ((), ()))):
    d = functools.partial(lax.dot_general, dimension_numbers=dims, preferred_element_type=F32)
    return d(ah, bh) + (d(ah, bl) + d(al, bh))


def prep_kernel(piece, field_ref, hi_ref, lo_ref, buf):
    w = field_ref.shape[1] // 8
    buf[...] = field_ref[...].T
    for p in range(8):
        v = buf[pl.ds(pl.multiple_of(piece[p] * w, 32), w), :]
        a = slice(p * w, (p + 1) * w)
        hi_ref[a, :], lo_ref[a, :] = split(v)


def prep(piece, field):
    rows, cols = field.shape
    tile = 128
    return pl.pallas_call(
        prep_kernel,
        grid=(rows // tile,),
        out_shape=[jax.ShapeDtypeStruct((cols, rows), BF)] * 2,
        in_specs=[pl.BlockSpec(memory_space=pltpu.SMEM), pl.BlockSpec((tile, cols), lambda n: (n, 0))],
        out_specs=[pl.BlockSpec((cols, tile), lambda n: (0, n))] * 2,
        scratch_shapes=[pltpu.VMEM((cols, tile), F32)],
        compiler_params=pltpu.CompilerParams(vmem_limit_bytes=16 << 20),
        cost_estimate=pl.CostEstimate(flops=0, bytes_accessed=rows * cols * 8, transcendentals=0),
        name="prep",
    )(piece, field)


def project_kernel(k, last, *refs):
    piece, block, b_ref, c_ref, hi_ref, lo_ref = refs[:6]
    prev = refs[6:6 + 2 * k]
    outs = refs[6 + 2 * k:]
    keep_ref, give_ref, vh_ref, vl_ref = outs[:4]
    vbuf = outs[-1]
    half = b_ref.shape[0]
    for p in range(16):
        src = b_ref if p < 8 else c_ref
        v = src[(p % 8) * (half // 8):(p % 8 + 1) * (half // 8), :]
        vbuf[pl.ds(pl.multiple_of(block[p] * (half // 8), 64), half // 8), :] = v
    vh_ref[...], vl_ref[...] = split(vbuf[...])
    vh, vl = vh_ref[...], vl_ref[...]
    w = hi_ref.shape[0] // 8
    r = w + 32 * k
    for h, out in ((1, give_ref), (0, keep_ref)):
        a = slice(h * 4 * w, (h + 1) * 4 * w)
        res = dot3(hi_ref[a, :], lo_ref[a, :], vh, vl)
        for p in range(4):
            out[p * r:p * r + w, :] = res[p * w:(p + 1) * w, :]
        for j in range(k):
            a = slice(h * 128, (h + 1) * 128)
            res = dot3(prev[2 * j][a, :], prev[2 * j + 1][a, :], vh, vl)
            for p in range(4):
                o = p * r + w + 32 * j
                out[o:o + 32, :] = res[p * 32:(p + 1) * 32, :]
    if not last:
        th_ref, tl_ref = outs[4:6]
        vt = vbuf[...].T
        vbuf[0:256, :] = vt[:, 0:256]
        vbuf[256:512, :] = vt[:, 256:512]
        vbuf[512:768, :] = vt[:, 512:768]
        vbuf[768:1024, :] = vt[:, 768:1024]
        for p in range(8):
            for m in range(4):
                v = vbuf[pl.ds(pl.multiple_of(m * 256 + piece[p] * 32, 32), 32), :]
                h, l = split(v)
                th_ref[p * 32:(p + 1) * 32, m * 256:(m + 1) * 256] = h
                tl_ref[p * 32:(p + 1) * 32, m * 256:(m + 1) * 256] = l


def project(k, piece, block, b, c, hi, lo, prev):
    last = k == NREF - 1
    rows, nb = 2 * b.shape[0], b.shape[1]
    cols = hi.shape[0]
    r = cols // 8 + 32 * k
    out = [jax.ShapeDtypeStruct((4 * r, nb), F32)] * 2 + [jax.ShapeDtypeStruct((rows, nb), BF)] * 2
    if not last:
        out += [jax.ShapeDtypeStruct((nb, rows), BF)] * 2
    vmem = pl.BlockSpec(memory_space=pltpu.VMEM)
    smem = pl.BlockSpec(memory_space=pltpu.SMEM)
    return pl.pallas_call(
        functools.partial(project_kernel, k, last),
        out_shape=out,
        in_specs=[smem, smem] + [vmem] * (4 + 2 * k),
        out_specs=[vmem] * len(out),
        scratch_shapes=[pltpu.VMEM((rows, nb), F32)],
        compiler_params=pltpu.CompilerParams(vmem_limit_bytes=24 << 20),
        cost_estimate=pl.CostEstimate(flops=6 * 8 * r * rows * nb, bytes_accessed=4 * rows * cols + 8 * rows * nb, transcendentals=0),
    )(piece, block, b, c, hi, lo, *prev)


def update_kernel(k, *refs):
    piece, own_ref, got_ref, vh_ref, vl_ref, t_ref, field_ref = refs[:7]
    prev = refs[7:7 + 2 * k]
    out_ref, sh_ref, sl_ref, wh_ref, wl_ref, g_ref, bh_ref, bl_ref = refs[7 + 2 * k:]
    n = pl.program_id(0)
    w = wh_ref.shape[0] // 8
    r = w + 32 * k
    last2 = (((1,), (1,)), ((), ()))

    @pl.when(n == 0)
    def _():
        for p in range(8):
            src = own_ref if p < 4 else got_ref
            o = (p % 4) * r
            q = piece[p]
            at = pl.ds(pl.multiple_of(q * w, 32), w)
            wh_ref[at, :], wl_ref[at, :] = split(src[o:o + w, :])
            for j in range(k):
                a = o + w + 32 * j
                g_ref[pl.ds(pl.multiple_of(j * 256 + q * 32, 32), 32), :] = src[a:a + 32, :]
        t = t_ref[...]
        at = lax.broadcasted_iota(jnp.int32, t.shape, 0)
        upto = lax.broadcasted_iota(jnp.int32, t.shape, 1)
        t = jnp.where(at <= upto, t, 0.0)
        bh_ref[0:256, :], bl_ref[0:256, :] = split(t.T)
        if k:
            th, tl = split(t)
            gh, gl = split(g_ref[0:256 * k, :])
            a = slice(256, 256 * (k + 1))
            bh_ref[a, :], bl_ref[a, :] = split(-dot3(gh, gl, th, tl, last2))
        b = slice(0, 256 * (k + 1))
        ah = jnp.concatenate([wh_ref[...]] + [v[...] for v in prev[0::2]], axis=1)
        al = jnp.concatenate([wl_ref[...]] + [v[...] for v in prev[1::2]], axis=1)
        sh_ref[...], sl_ref[...] = split(dot3(ah, al, bh_ref[b, :], bl_ref[b, :]))

    tile = field_ref.shape[1]
    a = pl.ds(pl.multiple_of(n * tile, tile), tile)
    out_ref[...] = field_ref[...] - dot3(vh_ref[...], vl_ref[...], sh_ref[a, :], sl_ref[a, :], last2)


def update(k, piece, own, got, vh, vl, t, field, prev):
    rows, cols = field.shape
    nb = vh.shape[1]
    tile = 256
    full = lambda a: pl.BlockSpec(a.shape, lambda n: (0, 0))
    smem = pl.BlockSpec(memory_space=pltpu.SMEM)
    cut = pl.BlockSpec((rows, tile), lambda n: (0, n))
    sdef = jax.ShapeDtypeStruct((cols, nb), BF)
    scratch = [(cols, nb, BF)] * 2 + [(512, nb, F32)] + [(768, nb, BF)] * 2
    return pl.pallas_call(
        functools.partial(update_kernel, k),
        grid=(cols // tile,),
        out_shape=[jax.ShapeDtypeStruct(field.shape, F32), sdef, sdef],
        in_specs=[smem, full(own), full(got), full(vh), full(vl), full(t), cut] + [full(a) for a in prev],
        out_specs=[cut, full(sdef), full(sdef)],
        scratch_shapes=[pltpu.VMEM(s[:2], s[2]) for s in scratch],
        compiler_params=pltpu.CompilerParams(vmem_limit_bytes=32 << 20),
        cost_estimate=pl.CostEstimate(flops=6 * rows * cols * nb, bytes_accessed=8 * rows * cols, transcendentals=0),
    )(piece, own, got, vh, vl, t, field, *prev)


def steps(eigvec, panels, factors):
    piece_t, block_t = tables()
    row, col = lax.axis_index("row"), lax.axis_index("col")
    piece = jnp.asarray(piece_t)[row]
    block = jnp.asarray(block_t)[row % 2, col]

    def spread(v):
        return [v] + [send(v, ZL[d]) for d in (1, 2, 3)]

    first = spread(panels[0])
    rest = spread(panels[1:])
    hi, lo = prep(piece, eigvec)
    vs, ts, ws = [], [], []
    for k in range(NREF):
        a = jnp.concatenate(first if k == 0 else [v[k - 1] for v in rest], axis=0)
        b = send(a, X1)
        b = jnp.concatenate([a, b], axis=0)
        c = send(b, X2)
        keep, give, vh, vl, *t = project(k, piece, block, b, c, hi, lo, [u for pair in ts for u in pair])
        vs.append((vh, vl))
        if t:
            ts.append(t)
        w = send(give, CORE)
        w = keep + w
        h = w.shape[0] // 2
        u = send(w[h:], Y1)
        w = w[:h] + u
        u = send(w[h // 2:], Y2)
        w = w[:h // 2] + u
        u = send(w, ZH)
        w = w + u
        u = send(w, Y2)
        w = jnp.concatenate([w, u], axis=0)
        u = send(w, Y1)
        w = jnp.concatenate([w, u], axis=0)
        ws.append((w, send(w, CORE)))
    field = eigvec
    ss = []
    for k in range(NREF):
        field, *s = update(k, piece, *ws[k], *vs[k], factors[k], field, [u for pair in ss for u in pair])
        ss.append(s)
    return field


def solution(mesh):
    in_specs = (P("row", "col"), P(None, ("row", "col"), None), P())
    out_specs = P("row", "col")
    return jax.shard_map(steps, mesh=mesh, in_specs=in_specs, out_specs=out_specs, check_vma=False)
```

profile of v0, /device:TPU:33, one launch (start us, length us, event | category | flops | bytes accessed | tf_op | source)
XLA Modules:
  0.0 153.9 jit_solution(13587385680111510823)
XLA Ops:
  5.0 2.4 %collective-permute-start.7 = (f32[64,256]{1,0:T(8,128)S(1)}, f32[64,256]{1,0:T(8,128)S(1)}, u32[]{:S(2)}, u32[]{:S(2)}) collective-permute-start(f32[64,256]{1,0:T(8,128)S(1)} %get-tuple-element.60), channel_id=1, source_target_pairs={{0,3},{1,2},{2,1},{3,0},{4,7},{5,6},{6,5},{7,4},{8,11},{9,10},{10,... | collective-permute-start | bytes 196616 | tf_op jit(solution)/shard_map/ppermute | solution.py:46
  9.6 8.5 %collective-permute-done.7 = f32[64,256]{1,0:T(8,128)S(1)} collective-permute-done((f32[64,256]{1,0:T(8,128)S(1)}, f32[64,256]{1,0:T(8,128)S(1)}, u32[]{:S(2)}, u32[]{:S(2)}) %collective-permute-start.7) | collective-permute-done | bytes 65568 | tf_op jit(solution)/shard_map/ppermute | solution.py:46
  18.9 2.6 %collective-permute-start.8 = (f32[256,256]{1,0:T(8,128)S(1)}, f32[256,256]{1,0:T(8,128)S(1)}, u32[]{:S(2)}, u32[]{:S(2)}) collective-permute-start(f32[256,256]{1,0:T(8,128)S(1)} %pad_maximum_fusion.7), channel_id=1, source_target_pairs={{0,4},{1,5},{2,6},{3,7},{4,0},{5,1},{6,2},{7,3},{8,12},{9,13},{10,... | collective-permute-start | bytes 786440 | tf_op jit(solution)/shard_map/ppermute | solution.py:46
  21.9 2.6 %collective-permute-start.3 = (f32[256,256]{1,0:T(8,128)S(1)}, f32[256,256]{1,0:T(8,128)S(1)}, u32[]{:S(2)}, u32[]{:S(2)}) collective-permute-start(f32[256,256]{1,0:T(8,128)S(1)} %pad_maximum_fusion.6), channel_id=1, source_target_pairs={{0,4},{1,5},{2,6},{3,7},{4,0},{5,1},{6,2},{7,3},{8,12},{9,13},{10,... | collective-permute-start | bytes 786440 | tf_op jit(solution)/shard_map/ppermute | solution.py:46
  25.8 5.4 %collective-permute-done.10 = f32[256,256]{1,0:T(8,128)S(1)} collective-permute-done((f32[256,256]{1,0:T(8,128)S(1)}, f32[256,256]{1,0:T(8,128)S(1)}, u32[]{:S(2)}, u32[]{:S(2)}) %collective-permute-start.10) | collective-permute-done | bytes 262176 | tf_op jit(solution)/shard_map/ppermute | solution.py:46
  32.4 2.5 %copy-done = f32[1024,1280]{1,0:T(8,128)S(1)} copy-done((f32[1024,1280]{1,0:T(8,128)S(1)}, f32[1024,1280]{1,0:T(8,128)}, u32[]{:S(2)}) %copy-start) | copy-done | bytes 5242904
  34.9 4.6 %prep.1 = (bf16[1280,1024]{1,0:T(8,128)(2,1)S(1)}, bf16[1280,1024]{1,0:T(8,128)(2,1)S(1)}) custom-call(s32[8]{0:T(128)S(1)} %dynamic-slice_bitcast_fusion.1.piece.refs_0_, f32[1024,1280]{1,0:T(8,128)S(1)} %copy-done), custom_call_target="tpu_custom_call" | custom-call | bytes 10485760 | tf_op jit(solution)/shard_map/prep/pallas_call | solution.py:91
  41.4 2.8 %shard_map.55 = (f32[640,256]{1,0:T(8,128)S(1)}, f32[640,256]{1,0:T(8,128)S(1)}, bf16[1024,256]{1,0:T(8,128)(2,1)S(1)}, bf16[1024,256]{1,0:T(8,128)(2,1)S(1)}, b...) custom-call(s32[8]{0:T(128)S(1)} %dynamic-slice_bitcast_fusion.1.piece.refs_0_, ...), custom_call_target="tpu_custom_call" | custom-call | flops 2013265920 | bytes 7340032 | tf_op jit(solution)/shard_map/pallas_call | solution.py:155
  44.3 10.9 %collective-permute-start.26 = (f32[640,256]{1,0:T(8,128)S(1)}, f32[640,256]{1,0:T(8,128)S(1)}, u32[]{:S(2)}, u32[]{:S(2)}) collective-permute-start(f32[640,256]{1,0:T(8,128)S(1)} %get-tuple-element.45), channel_id=1, source_target_pairs={{0,16},{1,17},{2,18},{3,19},{4,20},{5,21},{6,22},{7,23},{8,24},{9,... | collective-permute-start | bytes 1966088 | tf_op jit(solution)/shard_map/ppermute | solution.py:46
  55.2 3.4 %shard_map.56 = (f32[768,256]{1,0:T(8,128)S(1)}, f32[768,256]{1,0:T(8,128)S(1)}, bf16[1024,256]{1,0:T(8,128)(2,1)S(1)}, bf16[1024,256]{1,0:T(8,128)(2,1)S(1)}, b...) custom-call(s32[8]{0:T(128)S(1)} %dynamic-slice_bitcast_fusion.1.piece.refs_0_, ...), custom_call_target="tpu_custom_call" | custom-call | flops 2415919104 | bytes 7340032 | tf_op jit(solution)/shard_map/pallas_call | solution.py:155
  58.9 3.7 %shard_map.57 = (f32[896,256]{1,0:T(8,128)S(1)}, f32[896,256]{1,0:T(8,128)S(1)}, bf16[1024,256]{1,0:T(8,128)(2,1)S(1)}, bf16[1024,256]{1,0:T(8,128)(2,1)S(1)}) custom-call(s32[8]{0:T(128)S(1)} %dynamic-slice_bitcast_fusion.1.piece.refs_0_, s32[16]{0:T(128)S(1)} %dynamic-slice_bitcast_fusion.refs_1_, ...), custom_call_target="tpu_custom_call" | custom-call | flops 2818572288 | bytes 7340032 | tf_op jit(solution)/shard_map/pallas_call | solution.py:155
  62.6 2.7 %collective-permute-start.12 = (f32[896,256]{1,0:T(8,128)S(1)}, f32[896,256]{1,0:T(8,128)S(1)}, u32[]{:S(2)}, u32[]{:S(2)}) collective-permute-start(f32[896,256]{1,0:T(8,128)S(1)} %get-tuple-element.37), channel_id=1, source_target_pairs={{0,16},{1,17},{2,18},{3,19},{4,20},{5,21},{6,22},{7,23},{8,24},{9,... | collective-permute-start | bytes 2752520 | tf_op jit(solution)/shard_map/ppermute | solution.py:46
  65.4 2.8 %collective-permute-start.27 = (f32[320,256]{1,0:T(8,128)S(1)}, f32[320,256]{1,0:T(8,128)S(1)}, u32[]{:S(2)}, u32[]{:S(2)}) collective-permute-start(f32[320,256]{1,0:T(8,128)S(1)} %slice.117), channel_id=1, source_target_pairs={{0,64},{1,65},{2,66},{3,67},{4,68},{5,69},{6,70},{7,71},{8,72},{9,... | collective-permute-start | bytes 983048 | tf_op jit(solution)/shard_map/ppermute | solution.py:46
  68.2 4.5 %collective-permute-done.27 = f32[320,256]{1,0:T(8,128)S(1)} collective-permute-done((f32[320,256]{1,0:T(8,128)S(1)}, f32[320,256]{1,0:T(8,128)S(1)}, u32[]{:S(2)}, u32[]{:S(2)}) %collective-permute-start.27) | collective-permute-done | bytes 327712 | tf_op jit(solution)/shard_map/ppermute | solution.py:46
  73.3 2.5 %collective-permute-start.20 = (f32[384,256]{1,0:T(8,128)S(1)}, f32[384,256]{1,0:T(8,128)S(1)}, u32[]{:S(2)}, u32[]{:S(2)}) collective-permute-start(f32[384,256]{1,0:T(8,128)S(1)} %slice.113), channel_id=1, source_target_pairs={{0,64},{1,65},{2,66},{3,67},{4,68},{5,69},{6,70},{7,71},{8,72},{9,... | collective-permute-start | bytes 1179656 | tf_op jit(solution)/shard_map/ppermute | solution.py:46
  77.3 5.9 %collective-permute-start.29 = (f32[160,256]{1,0:T(8,128)S(1)}, f32[160,256]{1,0:T(8,128)S(1)}, u32[]{:S(2)}, u32[]{:S(2)}) collective-permute-start(f32[160,256]{1,0:T(8,128)S(1)} %slice_add_fusion.5), channel_id=1, source_target_pairs={{0,32},{1,33},{2,34},{3,35},{4,36},{5,37},{6,38},{7,39},{8,40},{9,... | collective-permute-start | bytes 491528 | tf_op jit(solution)/shard_map/ppermute | solution.py:46
  83.7 4.0 %collective-permute-done.13 = f32[448,256]{1,0:T(8,128)S(1)} collective-permute-done((f32[448,256]{1,0:T(8,128)S(1)}, f32[448,256]{1,0:T(8,128)S(1)}, u32[]{:S(2)}, u32[]{:S(2)}) %collective-permute-start.13) | collective-permute-done | bytes 458784 | tf_op jit(solution)/shard_map/ppermute | solution.py:46
  88.3 2.1 %collective-permute-done.21 = f32[192,256]{1,0:T(8,128)S(1)} collective-permute-done((f32[192,256]{1,0:T(8,128)S(1)}, f32[192,256]{1,0:T(8,128)S(1)}, u32[]{:S(2)}, u32[]{:S(2)}) %collective-permute-start.21) | collective-permute-done | bytes 196640 | tf_op jit(solution)/shard_map/ppermute | solution.py:46
  90.4 5.5 %collective-permute-start.22 = (f32[192,256]{1,0:T(8,128)S(1)}, f32[192,256]{1,0:T(8,128)S(1)}, u32[]{:S(2)}, u32[]{:S(2)}) collective-permute-start(f32[192,256]{1,0:T(8,128)S(1)} %slice_add_fusion.4), channel_id=1, source_target_pairs={{0,32},{1,33},{2,34},{3,35},{4,36},{5,37},{6,38},{7,39},{8,40},{9,... | collective-permute-start | bytes 589832 | tf_op jit(solution)/shard_map/ppermute | solution.py:46
  95.9 3.7 %collective-permute-start.15 = (f32[224,256]{1,0:T(8,128)S(1)}, f32[224,256]{1,0:T(8,128)S(1)}, u32[]{:S(2)}, u32[]{:S(2)}) collective-permute-start(f32[224,256]{1,0:T(8,128)S(1)} %slice_add_fusion.3), channel_id=1, source_target_pairs={{0,32},{1,33},{2,34},{3,35},{4,36},{5,37},{6,38},{7,39},{8,40},{9,... | collective-permute-start | bytes 688136 | tf_op jit(solution)/shard_map/ppermute | solution.py:46
  100.7 3.0 %collective-permute-done.22 = f32[192,256]{1,0:T(8,128)S(1)} collective-permute-done((f32[192,256]{1,0:T(8,128)S(1)}, f32[192,256]{1,0:T(8,128)S(1)}, u32[]{:S(2)}, u32[]{:S(2)}) %collective-permute-start.22) | collective-permute-done | bytes 196640 | tf_op jit(solution)/shard_map/ppermute | solution.py:46
  103.7 6.0 %collective-permute-start.23 = (f32[192,256]{1,0:T(8,128)S(1)}, f32[192,256]{1,0:T(8,128)S(1)}, u32[]{:S(2)}, u32[]{:S(2)}) collective-permute-start(f32[192,256]{1,0:T(8,128)S(1)} %add.60), channel_id=1, source_target_pairs={{0,192},{1,193},{2,194},{3,195},{4,196},{5,197},{6,198},{7,199},{8... | collective-permute-start | bytes 589832 | tf_op jit(solution)/shard_map/ppermute | solution.py:46
  109.7 2.8 %collective-permute-done.15 = f32[224,256]{1,0:T(8,128)S(1)} collective-permute-done((f32[224,256]{1,0:T(8,128)S(1)}, f32[224,256]{1,0:T(8,128)S(1)}, u32[]{:S(2)}, u32[]{:S(2)}) %collective-permute-start.15) | collective-permute-done | bytes 229408 | tf_op jit(solution)/shard_map/ppermute | solution.py:46
  112.5 2.1 %collective-permute-start.16 = (f32[224,256]{1,0:T(8,128)S(1)}, f32[224,256]{1,0:T(8,128)S(1)}, u32[]{:S(2)}, u32[]{:S(2)}) collective-permute-start(f32[224,256]{1,0:T(8,128)S(1)} %add.56), channel_id=1, source_target_pairs={{0,192},{1,193},{2,194},{3,195},{4,196},{5,197},{6,198},{7,199},{8... | collective-permute-start | bytes 688136 | tf_op jit(solution)/shard_map/ppermute | solution.py:46
  114.7 3.3 %collective-permute-start.31 = (f32[320,256]{1,0:T(8,128)S(1)}, f32[320,256]{1,0:T(8,128)S(1)}, u32[]{:S(2)}, u32[]{:S(2)}) collective-permute-start(f32[320,256]{1,0:T(8,128)S(1)} %pad_maximum_fusion.5), channel_id=1, source_target_pairs={{0,64},{1,65},{2,66},{3,67},{4,68},{5,69},{6,70},{7,71},{8,72},{9,... | collective-permute-start | bytes 983048 | tf_op jit(solution)/shard_map/ppermute | solution.py:46
  118.4 4.0 %collective-permute-start.17 = (f32[448,256]{1,0:T(8,128)S(1)}, f32[448,256]{1,0:T(8,128)S(1)}, u32[]{:S(2)}, u32[]{:S(2)}) collective-permute-start(f32[448,256]{1,0:T(8,128)S(1)} %pad_maximum_fusion.3), channel_id=1, source_target_pairs={{0,64},{1,65},{2,66},{3,67},{4,68},{5,69},{6,70},{7,71},{8,72},{9,... | collective-permute-start | bytes 1376264 | tf_op jit(solution)/shard_map/ppermute | solution.py:46
  122.4 2.5 %collective-permute-done.31 = f32[320,256]{1,0:T(8,128)S(1)} collective-permute-done((f32[320,256]{1,0:T(8,128)S(1)}, f32[320,256]{1,0:T(8,128)S(1)}, u32[]{:S(2)}, u32[]{:S(2)}) %collective-permute-start.31) | collective-permute-done | bytes 327712 | tf_op jit(solution)/shard_map/ppermute | solution.py:46
  125.3 3.8 %collective-permute-done.24 = f32[384,256]{1,0:T(8,128)S(1)} collective-permute-done((f32[384,256]{1,0:T(8,128)S(1)}, f32[384,256]{1,0:T(8,128)S(1)}, u32[]{:S(2)}, u32[]{:S(2)}) %collective-permute-start.24) | collective-permute-done | bytes 393248 | tf_op jit(solution)/shard_map/ppermute | solution.py:46
  129.4 4.5 %collective-permute-done.17 = f32[448,256]{1,0:T(8,128)S(1)} collective-permute-done((f32[448,256]{1,0:T(8,128)S(1)}, f32[448,256]{1,0:T(8,128)S(1)}, u32[]{:S(2)}, u32[]{:S(2)}) %collective-permute-start.17) | collective-permute-done | bytes 458784 | tf_op jit(solution)/shard_map/ppermute | solution.py:46
  134.5 5.3 %shard_map.58 = (f32[1024,1280]{1,0:T(8,128)S(1)}, bf16[1280,256]{1,0:T(8,128)(2,1)S(1)}, bf16[1280,256]{1,0:T(8,128)(2,1)S(1)}) custom-call(s32[8]{0:T(128)S(1)} %dynamic-slice_bitcast_fusion.1.piece.refs_0_, f32[640,256]{1,0:T(8,128)S(1)} %pad_maximum_fusion.2.refs_1_, f32[640,256]{1,0:T(8,128)S(1)} %collective-permute-done.32.refs_2_, ...), custom_call_target="tpu_custom_call" | custom-call | flops 2013265920 | bytes 10485760 | tf_op jit(solution)/shard_map/pallas_call | solution.py:215
  139.8 6.1 %shard_map.59 = (f32[1024,1280]{1,0:T(8,128)S(1)}, bf16[1280,256]{1,0:T(8,128)(2,1)S(1)}, bf16[1280,256]{1,0:T(8,128)(2,1)S(1)}) custom-call(s32[8]{0:T(128)S(1)} %dynamic-slice_bitcast_fusion.1.piece.refs_0_, f32[768,256]{1,0:T(8,128)S(1)} %pad_maximum_fusion.1.refs_1_, f32[768,256]{1,0:T(8,128)S(1)} %collective-permute-done.25.refs_2_, ...), custom_call_target="tpu_custom_call" | custom-call | flops 2013265920 | bytes 10485760 | tf_op jit(solution)/shard_map/pallas_call | solution.py:215
  145.9 8.0 %shard_map.60 = (f32[1024,1280]{1,0:T(8,128)}, bf16[1280,256]{1,0:T(8,128)(2,1)}, bf16[1280,256]{1,0:T(8,128)(2,1)}) custom-call(s32[8]{0:T(128)S(1)} %dynamic-slice_bitcast_fusion.1.piece.refs_0_, f32[896,256]{1,0:T(8,128)S(1)} %pad_maximum_fusion.refs_1_, f32[896,256]{1,0:T(8,128)S(1)} %collective-permute-done.18.refs_2_, ...), custom_call_target="tpu_custom_call" | custom-call | flops 2013265920 | bytes 10485760 | tf_op jit(solution)/shard_map/pallas_call | solution.py:215
  (95 shorter events, 19.2 us)
Async XLA Ops:
  0.9 20.6 %collective-permute-start.2 = (f32[2,64,256]{2,1,0:T(8,128)S(1)}, f32[2,64,256]{2,1,0:T(8,128)S(1)}, u32[]{:S(2)}, u32[]{:S(2)}) collective-permute-start(f32[2,64,256]{2,1,0:T(8,128)S(1)} %slice.78), channel_id=1, source_target_pairs={{0,3},{1,2},{2,1},{3,0},{4,7},{5,6},{6,5},{7,4},{8,11},{9,10},{10,... | collective-permute-start | bytes 393224 | tf_op jit(solution)/shard_map/ppermute | solution.py:46
  2.6 18.9 %collective-permute-start.1 = (f32[2,64,256]{2,1,0:T(8,128)S(1)}, f32[2,64,256]{2,1,0:T(8,128)S(1)}, u32[]{:S(2)}, u32[]{:S(2)}) collective-permute-start(f32[2,64,256]{2,1,0:T(8,128)S(1)} %slice.78), channel_id=1, source_target_pairs={{0,2},{1,3},{2,0},{3,1},{4,6},{5,7},{6,4},{7,5},{8,10},{9,11},{10,... | collective-permute-start | bytes 393224 | tf_op jit(solution)/shard_map/ppermute | solution.py:46
  5.0 13.1 %collective-permute-start.7 = (f32[64,256]{1,0:T(8,128)S(1)}, f32[64,256]{1,0:T(8,128)S(1)}, u32[]{:S(2)}, u32[]{:S(2)}) collective-permute-start(f32[64,256]{1,0:T(8,128)S(1)} %get-tuple-element.60), channel_id=1, source_target_pairs={{0,3},{1,2},{2,1},{3,0},{4,7},{5,6},{6,5},{7,4},{8,11},{9,10},{10,... | collective-permute-start | bytes 196616 | tf_op jit(solution)/shard_map/ppermute | solution.py:46
  7.4 11.5 %collective-permute-start.6 = (f32[64,256]{1,0:T(8,128)S(1)}, f32[64,256]{1,0:T(8,128)S(1)}, u32[]{:S(2)}, u32[]{:S(2)}) collective-permute-start(f32[64,256]{1,0:T(8,128)S(1)} %get-tuple-element.60), channel_id=1, source_target_pairs={{0,2},{1,3},{2,0},{3,1},{4,6},{5,7},{6,4},{7,5},{8,10},{9,11},{10,... | collective-permute-start | bytes 196616 | tf_op jit(solution)/shard_map/ppermute | solution.py:46
  8.3 10.6 %collective-permute-start.5 = (f32[64,256]{1,0:T(8,128)S(1)}, f32[64,256]{1,0:T(8,128)S(1)}, u32[]{:S(2)}, u32[]{:S(2)}) collective-permute-start(f32[64,256]{1,0:T(8,128)S(1)} %get-tuple-element.60), channel_id=1, source_target_pairs={{0,1},{1,0},{2,3},{3,2},{4,5},{5,4},{6,7},{7,6},{8,9},{9,8},{10,11... | collective-permute-start | bytes 196616 | tf_op jit(solution)/shard_map/ppermute | solution.py:46
  18.9 6.5 %collective-permute-start.8 = (f32[256,256]{1,0:T(8,128)S(1)}, f32[256,256]{1,0:T(8,128)S(1)}, u32[]{:S(2)}, u32[]{:S(2)}) collective-permute-start(f32[256,256]{1,0:T(8,128)S(1)} %pad_maximum_fusion.7), channel_id=1, source_target_pairs={{0,4},{1,5},{2,6},{3,7},{4,0},{5,1},{6,2},{7,3},{8,12},{9,13},{10,... | collective-permute-start | bytes 786440 | tf_op jit(solution)/shard_map/ppermute | solution.py:46
  21.9 17.5 %collective-permute-start.3 = (f32[256,256]{1,0:T(8,128)S(1)}, f32[256,256]{1,0:T(8,128)S(1)}, u32[]{:S(2)}, u32[]{:S(2)}) collective-permute-start(f32[256,256]{1,0:T(8,128)S(1)} %pad_maximum_fusion.6), channel_id=1, source_target_pairs={{0,4},{1,5},{2,6},{3,7},{4,0},{5,1},{6,2},{7,3},{8,12},{9,13},{10,... | collective-permute-start | bytes 786440 | tf_op jit(solution)/shard_map/ppermute | solution.py:46
  24.5 6.7 %collective-permute-start.10 = (f32[256,256]{1,0:T(8,128)S(1)}, f32[256,256]{1,0:T(8,128)S(1)}, u32[]{:S(2)}, u32[]{:S(2)}) collective-permute-start(f32[256,256]{1,0:T(8,128)S(1)} %pad_maximum_fusion.8), channel_id=1, source_target_pairs={{0,4},{1,5},{2,6},{3,7},{4,0},{5,1},{6,2},{7,3},{8,12},{9,13},{10,... | collective-permute-start | bytes 786440 | tf_op jit(solution)/shard_map/ppermute | solution.py:46
  25.4 16.0 %collective-permute-start.9 = (f32[512,256]{1,0:T(8,128)S(1)}, f32[512,256]{1,0:T(8,128)S(1)}, u32[]{:S(2)}, u32[]{:S(2)}) collective-permute-start(f32[512,256]{1,0:T(8,128)S(1)} %constant_dynamic-update-slice_fusion.5.refs_2_), channel_id=1, source_target_pairs={{0,12},{1,13},{2,14},{3,15},{4,8},{5,9},{6,10},{7,11},{8,4},{9,5},... | collective-permute-start | bytes 1572872 | tf_op jit(solution)/shard_map/ppermute | solution.py:46
  31.3 23.9 %collective-permute-start.11 = (f32[512,256]{1,0:T(8,128)S(1)}, f32[512,256]{1,0:T(8,128)S(1)}, u32[]{:S(2)}, u32[]{:S(2)}) collective-permute-start(f32[512,256]{1,0:T(8,128)S(1)} %constant_dynamic-update-slice_fusion.10.refs_2_), channel_id=1, source_target_pairs={{0,12},{1,13},{2,14},{3,15},{4,8},{5,9},{6,10},{7,11},{8,4},{9,5},... | collective-permute-start | bytes 1572872 | tf_op jit(solution)/shard_map/ppermute | solution.py:46
  39.5 19.4 %collective-permute-start.4 = (f32[512,256]{1,0:T(8,128)S(1)}, f32[512,256]{1,0:T(8,128)S(1)}, u32[]{:S(2)}, u32[]{:S(2)}) collective-permute-start(f32[512,256]{1,0:T(8,128)S(1)} %constant_dynamic-update-slice_fusion.refs_2_), channel_id=1, source_target_pairs={{0,12},{1,13},{2,14},{3,15},{4,8},{5,9},{6,10},{7,11},{8,4},{9,5},... | collective-permute-start | bytes 1572872 | tf_op jit(solution)/shard_map/ppermute | solution.py:46
  44.3 21.0 %collective-permute-start.26 = (f32[640,256]{1,0:T(8,128)S(1)}, f32[640,256]{1,0:T(8,128)S(1)}, u32[]{:S(2)}, u32[]{:S(2)}) collective-permute-start(f32[640,256]{1,0:T(8,128)S(1)} %get-tuple-element.45), channel_id=1, source_target_pairs={{0,16},{1,17},{2,18},{3,19},{4,20},{5,21},{6,22},{7,23},{8,24},{9,... | collective-permute-start | bytes 1966088 | tf_op jit(solution)/shard_map/ppermute | solution.py:46
  58.6 14.6 %collective-permute-start.19 = (f32[768,256]{1,0:T(8,128)S(1)}, f32[768,256]{1,0:T(8,128)S(1)}, u32[]{:S(2)}, u32[]{:S(2)}) collective-permute-start(f32[768,256]{1,0:T(8,128)S(1)} %get-tuple-element.41), channel_id=1, source_target_pairs={{0,16},{1,17},{2,18},{3,19},{4,20},{5,21},{6,22},{7,23},{8,24},{9,... | collective-permute-start | bytes 2359304 | tf_op jit(solution)/shard_map/ppermute | solution.py:46
  62.6 13.2 %collective-permute-start.12 = (f32[896,256]{1,0:T(8,128)S(1)}, f32[896,256]{1,0:T(8,128)S(1)}, u32[]{:S(2)}, u32[]{:S(2)}) collective-permute-start(f32[896,256]{1,0:T(8,128)S(1)} %get-tuple-element.37), channel_id=1, source_target_pairs={{0,16},{1,17},{2,18},{3,19},{4,20},{5,21},{6,22},{7,23},{8,24},{9,... | collective-permute-start | bytes 2752520 | tf_op jit(solution)/shard_map/ppermute | solution.py:46
  65.4 7.3 %collective-permute-start.27 = (f32[320,256]{1,0:T(8,128)S(1)}, f32[320,256]{1,0:T(8,128)S(1)}, u32[]{:S(2)}, u32[]{:S(2)}) collective-permute-start(f32[320,256]{1,0:T(8,128)S(1)} %slice.117), channel_id=1, source_target_pairs={{0,64},{1,65},{2,66},{3,67},{4,68},{5,69},{6,70},{7,71},{8,72},{9,... | collective-permute-start | bytes 983048 | tf_op jit(solution)/shard_map/ppermute | solution.py:46
  72.8 4.6 %collective-permute-start.28 = (f32[160,256]{1,0:T(8,128)S(1)}, f32[160,256]{1,0:T(8,128)S(1)}, u32[]{:S(2)}, u32[]{:S(2)}) collective-permute-start(f32[160,256]{1,0:T(8,128)S(1)} %slice.119), channel_id=1, source_target_pairs={{0,192},{1,193},{2,194},{3,195},{4,196},{5,197},{6,198},{7,199},{8... | collective-permute-start | bytes 491528 | tf_op jit(solution)/shard_map/ppermute | solution.py:46
  73.3 10.0 %collective-permute-start.20 = (f32[384,256]{1,0:T(8,128)S(1)}, f32[384,256]{1,0:T(8,128)S(1)}, u32[]{:S(2)}, u32[]{:S(2)}) collective-permute-start(f32[384,256]{1,0:T(8,128)S(1)} %slice.113), channel_id=1, source_target_pairs={{0,64},{1,65},{2,66},{3,67},{4,68},{5,69},{6,70},{7,71},{8,72},{9,... | collective-permute-start | bytes 1179656 | tf_op jit(solution)/shard_map/ppermute | solution.py:46
  75.9 11.8 %collective-permute-start.13 = (f32[448,256]{1,0:T(8,128)S(1)}, f32[448,256]{1,0:T(8,128)S(1)}, u32[]{:S(2)}, u32[]{:S(2)}) collective-permute-start(f32[448,256]{1,0:T(8,128)S(1)} %slice.109), channel_id=1, source_target_pairs={{0,64},{1,65},{2,66},{3,67},{4,68},{5,69},{6,70},{7,71},{8,72},{9,... | collective-permute-start | bytes 1376264 | tf_op jit(solution)/shard_map/ppermute | solution.py:46
  77.3 22.3 %collective-permute-start.29 = (f32[160,256]{1,0:T(8,128)S(1)}, f32[160,256]{1,0:T(8,128)S(1)}, u32[]{:S(2)}, u32[]{:S(2)}) collective-permute-start(f32[160,256]{1,0:T(8,128)S(1)} %slice_add_fusion.5), channel_id=1, source_target_pairs={{0,32},{1,33},{2,34},{3,35},{4,36},{5,37},{6,38},{7,39},{8,40},{9,... | collective-permute-start | bytes 491528 | tf_op jit(solution)/shard_map/ppermute | solution.py:46
  83.3 7.0 %collective-permute-start.21 = (f32[192,256]{1,0:T(8,128)S(1)}, f32[192,256]{1,0:T(8,128)S(1)}, u32[]{:S(2)}, u32[]{:S(2)}) collective-permute-start(f32[192,256]{1,0:T(8,128)S(1)} %slice.115), channel_id=1, source_target_pairs={{0,192},{1,193},{2,194},{3,195},{4,196},{5,197},{6,198},{7,199},{8... | collective-permute-start | bytes 589832 | tf_op jit(solution)/shard_map/ppermute | solution.py:46
  87.8 8.0 %collective-permute-start.14 = (f32[224,256]{1,0:T(8,128)S(1)}, f32[224,256]{1,0:T(8,128)S(1)}, u32[]{:S(2)}, u32[]{:S(2)}) collective-permute-start(f32[224,256]{1,0:T(8,128)S(1)} %slice.111), channel_id=1, source_target_pairs={{0,192},{1,193},{2,194},{3,195},{4,196},{5,197},{6,198},{7,199},{8... | collective-permute-start | bytes 688136 | tf_op jit(solution)/shard_map/ppermute | solution.py:46
  90.4 13.3 %collective-permute-start.22 = (f32[192,256]{1,0:T(8,128)S(1)}, f32[192,256]{1,0:T(8,128)S(1)}, u32[]{:S(2)}, u32[]{:S(2)}) collective-permute-start(f32[192,256]{1,0:T(8,128)S(1)} %slice_add_fusion.4), channel_id=1, source_target_pairs={{0,32},{1,33},{2,34},{3,35},{4,36},{5,37},{6,38},{7,39},{8,40},{9,... | collective-permute-start | bytes 589832 | tf_op jit(solution)/shard_map/ppermute | solution.py:46
  95.9 16.6 %collective-permute-start.15 = (f32[224,256]{1,0:T(8,128)S(1)}, f32[224,256]{1,0:T(8,128)S(1)}, u32[]{:S(2)}, u32[]{:S(2)}) collective-permute-start(f32[224,256]{1,0:T(8,128)S(1)} %slice_add_fusion.3), channel_id=1, source_target_pairs={{0,32},{1,33},{2,34},{3,35},{4,36},{5,37},{6,38},{7,39},{8,40},{9,... | collective-permute-start | bytes 688136 | tf_op jit(solution)/shard_map/ppermute | solution.py:46
  99.6 15.0 %collective-permute-start.30 = (f32[160,256]{1,0:T(8,128)S(1)}, f32[160,256]{1,0:T(8,128)S(1)}, u32[]{:S(2)}, u32[]{:S(2)}) collective-permute-start(f32[160,256]{1,0:T(8,128)S(1)} %add.64), channel_id=1, source_target_pairs={{0,192},{1,193},{2,194},{3,195},{4,196},{5,197},{6,198},{7,199},{8... | collective-permute-start | bytes 491528 | tf_op jit(solution)/shard_map/ppermute | solution.py:46
  103.7 14.2 %collective-permute-start.23 = (f32[192,256]{1,0:T(8,128)S(1)}, f32[192,256]{1,0:T(8,128)S(1)}, u32[]{:S(2)}, u32[]{:S(2)}) collective-permute-start(f32[192,256]{1,0:T(8,128)S(1)} %add.60), channel_id=1, source_target_pairs={{0,192},{1,193},{2,194},{3,195},{4,196},{5,197},{6,198},{7,199},{8... | collective-permute-start | bytes 589832 | tf_op jit(solution)/shard_map/ppermute | solution.py:46
  112.5 5.8 %collective-permute-start.16 = (f32[224,256]{1,0:T(8,128)S(1)}, f32[224,256]{1,0:T(8,128)S(1)}, u32[]{:S(2)}, u32[]{:S(2)}) collective-permute-start(f32[224,256]{1,0:T(8,128)S(1)} %add.56), channel_id=1, source_target_pairs={{0,192},{1,193},{2,194},{3,195},{4,196},{5,197},{6,198},{7,199},{8... | collective-permute-start | bytes 688136 | tf_op jit(solution)/shard_map/ppermute | solution.py:46
  114.7 10.2 %collective-permute-start.31 = (f32[320,256]{1,0:T(8,128)S(1)}, f32[320,256]{1,0:T(8,128)S(1)}, u32[]{:S(2)}, u32[]{:S(2)}) collective-permute-start(f32[320,256]{1,0:T(8,128)S(1)} %pad_maximum_fusion.5), channel_id=1, source_target_pairs={{0,64},{1,65},{2,66},{3,67},{4,68},{5,69},{6,70},{7,71},{8,72},{9,... | collective-permute-start | bytes 983048 | tf_op jit(solution)/shard_map/ppermute | solution.py:46
  118.0 11.1 %collective-permute-start.24 = (f32[384,256]{1,0:T(8,128)S(1)}, f32[384,256]{1,0:T(8,128)S(1)}, u32[]{:S(2)}, u32[]{:S(2)}) collective-permute-start(f32[384,256]{1,0:T(8,128)S(1)} %pad_maximum_fusion.4), channel_id=1, source_target_pairs={{0,64},{1,65},{2,66},{3,67},{4,68},{5,69},{6,70},{7,71},{8,72},{9,... | collective-permute-start | bytes 1179656 | tf_op jit(solution)/shard_map/ppermute | solution.py:46
  118.4 15.6 %collective-permute-start.17 = (f32[448,256]{1,0:T(8,128)S(1)}, f32[448,256]{1,0:T(8,128)S(1)}, u32[]{:S(2)}, u32[]{:S(2)}) collective-permute-start(f32[448,256]{1,0:T(8,128)S(1)} %pad_maximum_fusion.3), channel_id=1, source_target_pairs={{0,64},{1,65},{2,66},{3,67},{4,68},{5,69},{6,70},{7,71},{8,72},{9,... | collective-permute-start | bytes 1376264 | tf_op jit(solution)/shard_map/ppermute | solution.py:46
  124.9 9.5 %collective-permute-start.32 = (f32[640,256]{1,0:T(8,128)S(1)}, f32[640,256]{1,0:T(8,128)S(1)}, u32[]{:S(2)}, u32[]{:S(2)}) collective-permute-start(f32[640,256]{1,0:T(8,128)S(1)} %pad_maximum_fusion.2.refs_1_), channel_id=1, source_target_pairs={{0,16},{1,17},{2,18},{3,19},{4,20},{5,21},{6,22},{7,23},{8,24},{9,... | collective-permute-start | bytes 1966088 | tf_op jit(solution)/shard_map/ppermute | solution.py:46
  129.1 10.7 %collective-permute-start.25 = (f32[768,256]{1,0:T(8,128)S(1)}, f32[768,256]{1,0:T(8,128)S(1)}, u32[]{:S(2)}, u32[]{:S(2)}) collective-permute-start(f32[768,256]{1,0:T(8,128)S(1)} %pad_maximum_fusion.1.refs_1_), channel_id=1, source_target_pairs={{0,16},{1,17},{2,18},{3,19},{4,20},{5,21},{6,22},{7,23},{8,24},{9,... | collective-permute-start | bytes 2359304 | tf_op jit(solution)/shard_map/ppermute | solution.py:46
  134.0 11.8 %collective-permute-start.18 = (f32[896,256]{1,0:T(8,128)S(1)}, f32[896,256]{1,0:T(8,128)S(1)}, u32[]{:S(2)}, u32[]{:S(2)}) collective-permute-start(f32[896,256]{1,0:T(8,128)S(1)} %pad_maximum_fusion.refs_1_), channel_id=1, source_target_pairs={{0,16},{1,17},{2,18},{3,19},{4,20},{5,21},{6,22},{7,23},{8,24},{9,... | collective-permute-start | bytes 2752520 | tf_op jit(solution)/shard_map/ppermute | solution.py:46
  (5 other events, 123.9 us)
where the time goes:
time: 154 us
  starting transfers between devices  67.7 us (44%)
  waiting for transfers between devices  44 us (29%)
  Pallas kernels  33.9 us (22%)
  local copies, waits for them, and re-layouts  6.94 us (5%)
    ppermute x33, starting transfers between devices, send(): return lax.ppermute(a, ('row', 'col'), perm)  67.7 us
    ppermute x33, waiting for transfers between devices, send(): return lax.ppermute(a, ('row', 'col'), perm)  44 us
    pallas_call x3, Pallas kernels, update(): pl.pallas_call(functools.partial(update_kernel, k), grid=(cols // tile,),...  19.4 us
    pallas_call x3, Pallas kernels, project(): pl.pallas_call(functools.partial(project_kernel, k, last), out_shape=out,...  9.95 us
    pallas_call x1, Pallas kernels, prep(): pl.pallas_call(prep_kernel, grid=(rows // tile,), out_shape=[jax.ShapeDty...  4.56 us
    unnamed x15, local copies, waits for them, and re-layouts  3.47 us
  transfers between devices with their start and end apart: 33, of which 15 were waited for; matrix products, arithmetic and copies ran while one was open for 3% of the time, Pallas kernels for 17%

commit v1 on v0

v1 whole, which is shorter than its diff:
```python
import functools

import jax
import jax.numpy as jnp
import numpy as np
from jax import lax
from jax.experimental import pallas as pl
from jax.experimental.pallas import tpu as pltpu
from jax.sharding import PartitionSpec as P


NREF = 3
BF = jnp.bfloat16
F32 = jnp.float32


def lin(y, zh, c, x, zl):
    return ((y * 2 + zh) * 2 + c) * 16 + x * 4 + zl


def xor_pair(core):
    return (1, 3) if core == 0 else (3, 1)


def perm_of(f):
    pairs = []
    for y in range(4):
        for zh in range(2):
            for c in range(2):
                for x in range(4):
                    for zl in range(4):
                        pairs.append((lin(y, zh, c, x, zl), lin(*f(y, zh, c, x, zl))))
    return pairs


CORE = perm_of(lambda y, zh, c, x, zl: (y, zh, 1 - c, x, zl))
Y1 = perm_of(lambda y, zh, c, x, zl: (y ^ xor_pair(c)[0], zh, c, x, zl))
Y2 = perm_of(lambda y, zh, c, x, zl: (y ^ xor_pair(c)[1], zh, c, x, zl))
X1 = perm_of(lambda y, zh, c, x, zl: (y, zh, c, x ^ xor_pair(c)[0], zl))
X2 = perm_of(lambda y, zh, c, x, zl: (y, zh, c, x ^ xor_pair(c)[1], zl))
ZH = perm_of(lambda y, zh, c, x, zl: (y, 1 - zh, c, x, zl))
ZL = [perm_of(lambda y, zh, c, x, zl, d=d: (y, zh, c, x, zl ^ d)) for d in range(4)]


def send(a, perm):
    return lax.ppermute(a, ("row", "col"), perm)


def tables():
    piece = np.zeros((16, 8), np.int32)
    block = np.zeros((2, 16, 2, 16), np.int32)
    for r in range(16):
        y, c = r // 4, r % 2
        for p in range(8):
            b0, b1, b2 = p // 4, (p // 2) % 2, p % 2
            owner = c ^ b0
            g = xor_pair(owner)
            piece[r, p] = owner * 4 + (y ^ (b1 * g[0]) ^ (b2 * g[1]))
    for c in range(2):
        g = xor_pair(c)
        for j in range(16):
            x, zl = j // 4, j % 4
            for p in range(16):
                b2, b1, zp = p // 8, (p // 4) % 2, p % 4
                block[c, j, 0, p] = (x ^ (b1 * g[0]) ^ (b2 * g[1])) * 4 + (zl ^ zp)
                zp, b2, b1 = p // 4, (p // 2) % 2, p % 2
                block[c, j, 1, p] = (x ^ (b1 * g[0]) ^ (b2 * g[1])) * 4 + (zl ^ zp)
    return piece, block


def split(v):
    hi = v.astype(BF)
    return hi, (v - hi.astype(F32)).astype(BF)


def dot3(ah, al, bh, bl, dims=(((1,), (0,)), ((), ()))):
    d = functools.partial(lax.dot_general, dimension_numbers=dims, preferred_element_type=F32)
    return d(ah, bh) + (d(ah, bl) + d(al, bh))


def prep_kernel(piece, field_ref, hi_ref, lo_ref, buf):
    w = field_ref.shape[1] // 8
    tile = buf.shape[-1]

    @pl.loop(0, field_ref.shape[0] // tile)
    def _(n):
        b = pl.ds(pl.multiple_of(n * tile, tile), tile)
        buf[...] = field_ref[b, :].T
        for p in range(8):
            v = buf[pl.ds(pl.multiple_of(piece[p] * w, 32), w), :]
            a = slice(p * w, (p + 1) * w)
            hi_ref[a, b], lo_ref[a, b] = split(v)


def prep(piece, field):
    rows, cols = field.shape
    return pl.pallas_call(
        prep_kernel,
        out_shape=[jax.ShapeDtypeStruct((cols, rows), BF)] * 2,
        in_specs=[pl.BlockSpec(memory_space=pltpu.SMEM), pl.BlockSpec(memory_space=pltpu.VMEM)],
        out_specs=[pl.BlockSpec(memory_space=pltpu.VMEM)] * 2,
        scratch_shapes=[pltpu.VMEM((cols, 256), F32)],
        compiler_params=pltpu.CompilerParams(vmem_limit_bytes=24 << 20),
        cost_estimate=pl.CostEstimate(flops=0, bytes_accessed=rows * cols * 8, transcendentals=0),
        name="prep",
    )(piece, field)


def project_kernel(k, last, parts, *refs):
    piece, block = refs[:2]
    blocks = refs[2:2 + parts]
    hi_ref, lo_ref = refs[2 + parts:4 + parts]
    prev = refs[4 + parts:4 + parts + 2 * k]
    outs = refs[4 + parts + 2 * k:]
    keep_ref, give_ref, vh_ref, vl_ref = outs[:4]
    vbuf = outs[-1]
    at = 0
    for src in blocks:
        for o in range(0, src.shape[0], 64):
            vbuf[pl.ds(pl.multiple_of(block[at] * 64, 64), 64), :] = src[o:o + 64, :]
            at += 1
    vh_ref[...], vl_ref[...] = split(vbuf[...])
    vh, vl = vh_ref[...], vl_ref[...]
    w = hi_ref.shape[0] // 8
    r = w + 32 * k

    def side(h, refs):
        a = pl.ds(pl.multiple_of(h * 4 * w, 32), 4 * w)
        res = dot3(hi_ref[a, :], lo_ref[a, :], vh, vl)
        a = pl.ds(pl.multiple_of(h * 128, 128), 128)
        more = [dot3(prev[2 * j][a, :], prev[2 * j + 1][a, :], vh, vl) for j in range(k)]

        def store(out):
            for p in range(4):
                out[p * r:p * r + w, :] = res[p * w:(p + 1) * w, :]
                for j in range(k):
                    o = p * r + w + 32 * j
                    out[o:o + 32, :] = more[j][p * 32:(p + 1) * 32, :]

        for g, out in refs:
            if len(refs) == 1:
                store(out)
            else:
                pl.when(h == g)(functools.partial(store, out))

    if k == 0:
        pl.loop(0, 2)(lambda h: side(h, ((0, keep_ref), (1, give_ref))))
    else:
        side(1, ((1, give_ref),))
        side(0, ((0, keep_ref),))
    if not last:
        th_ref, tl_ref = outs[4:6]
        vt = vbuf[...].T
        vbuf[0:256, :] = vt[:, 0:256]
        vbuf[256:512, :] = vt[:, 256:512]
        vbuf[512:768, :] = vt[:, 512:768]
        vbuf[768:1024, :] = vt[:, 768:1024]

        @pl.loop(0, 8)
        def _(p):
            to = pl.ds(pl.multiple_of(p * 32, 32), 32)
            for m in range(4):
                v = vbuf[pl.ds(pl.multiple_of(m * 256 + piece[p] * 32, 32), 32), :]
                b = slice(m * 256, (m + 1) * 256)
                th_ref[to, b], tl_ref[to, b] = split(v)


def project(k, piece, block, parts, hi, lo, prev):
    last = k == NREF - 1
    rows, nb = sum(v.shape[0] for v in parts), parts[0].shape[1]
    cols = hi.shape[0]
    r = cols // 8 + 32 * k
    out = [jax.ShapeDtypeStruct((4 * r, nb), F32)] * 2 + [jax.ShapeDtypeStruct((rows, nb), BF)] * 2
    if not last:
        out += [jax.ShapeDtypeStruct((nb, rows), BF)] * 2
    vmem = pl.BlockSpec(memory_space=pltpu.VMEM)
    smem = pl.BlockSpec(memory_space=pltpu.SMEM)
    return pl.pallas_call(
        functools.partial(project_kernel, k, last, len(parts)),
        out_shape=out,
        in_specs=[smem, smem] + [vmem] * (2 + len(parts) + 2 * k),
        out_specs=[vmem] * len(out),
        scratch_shapes=[pltpu.VMEM((rows, nb), F32)],
        compiler_params=pltpu.CompilerParams(vmem_limit_bytes=24 << 20),
        cost_estimate=pl.CostEstimate(flops=6 * 8 * r * rows * nb, bytes_accessed=4 * rows * cols + 8 * rows * nb, transcendentals=0),
    )(piece, block, *parts, hi, lo, *prev)


def update_kernel(k, last, *refs):
    piece, own_ref, got_ref, vh_ref, vl_ref, t_ref, field_ref = refs[:7]
    prev = refs[7:7 + 2 * k]
    if last:
        out_ref, wh_ref, wl_ref, g_ref, bh_ref, bl_ref, done, sems = refs[7 + 2 * k:]
    else:
        out_ref, sh_ref, sl_ref, wh_ref, wl_ref, g_ref, bh_ref, bl_ref = refs[7 + 2 * k:]
    cols = wh_ref.shape[0]
    w = cols // 8
    r = w + 32 * k
    last2 = (((1,), (1,)), ((), ()))
    t = t_ref[...]
    at = lax.broadcasted_iota(jnp.int32, t.shape, 0)
    upto = lax.broadcasted_iota(jnp.int32, t.shape, 1)
    t = jnp.where(at <= upto, t, 0.0)
    bh_ref[0:256, :], bl_ref[0:256, :] = split(t.T)
    for p in range(8):
        src = own_ref if p < 4 else got_ref
        for j in range(k):
            a = (p % 4) * r + w + 32 * j
            g_ref[pl.ds(pl.multiple_of(j * 256 + piece[p] * 32, 32), 32), :] = src[a:a + 32, :]
    if k:
        th, tl = split(t)
        gh, gl = split(g_ref[0:256 * k, :])
        a = slice(256, 256 * (k + 1))
        bh_ref[a, :], bl_ref[a, :] = split(-dot3(gh, gl, th, tl, last2))
    for base, src in ((0, own_ref), (4, got_ref)):

        def place(p, base=base, src=src):
            a = pl.ds(pl.multiple_of(piece[base + p] * w, 32), w)
            wh_ref[a, :], wl_ref[a, :] = split(src[pl.ds(pl.multiple_of(p * r, 32), w), :])

        if last:
            for p in range(4):
                place(p)
        else:
            pl.loop(0, 4)(place)
    b = slice(0, 256 * (k + 1))
    tile = 256

    def store(n):
        to = slice(n * tile, (n + 1) * tile)
        return pltpu.make_async_copy(done.at[n], out_ref.at[:, to], sems.at[n])

    def step(n):
        a = pl.ds(pl.multiple_of(n * tile, tile), tile) if k == 0 else slice(n * tile, (n + 1) * tile)
        ah = jnp.concatenate([wh_ref[a, :]] + [v[a, :] for v in prev[0::2]], axis=1)
        al = jnp.concatenate([wl_ref[a, :]] + [v[a, :] for v in prev[1::2]], axis=1)
        sh, sl = split(dot3(ah, al, bh_ref[b, :], bl_ref[b, :]))
        if not last:
            sh_ref[a, :], sl_ref[a, :] = sh, sl
        res = field_ref[:, a] - dot3(vh_ref[...], vl_ref[...], sh, sl, last2)
        if last:
            done[n] = res
            store(n).start()
        else:
            out_ref[:, a] = res

    if k == 0:
        pl.loop(0, cols // tile)(step)
    else:
        for n in range(cols // tile):
            step(n)
    if last:
        for n in range(cols // tile):
            store(n).wait()


def update(k, piece, own, got, vh, vl, t, field, prev):
    last = k == NREF - 1
    rows, cols = field.shape
    nb = vh.shape[1]
    smem = pl.BlockSpec(memory_space=pltpu.SMEM)
    vmem = pl.BlockSpec(memory_space=pltpu.VMEM)
    sdef = jax.ShapeDtypeStruct((cols, nb), BF)
    scratch = [(cols, nb, BF)] * 2 + [(512, nb, F32)] + [(768, nb, BF)] * 2
    scratch = [pltpu.VMEM(s[:2], s[2]) for s in scratch]
    if last:
        scratch += [pltpu.VMEM((cols // 256, rows, 256), F32), pltpu.SemaphoreType.DMA((cols // 256,))]
    return pl.pallas_call(
        functools.partial(update_kernel, k, last),
        out_shape=[jax.ShapeDtypeStruct(field.shape, F32)] + [sdef] * (0 if last else 2),
        in_specs=[smem] + [vmem] * (6 + len(prev)),
        out_specs=[pl.BlockSpec(memory_space=pltpu.HBM)] if last else [vmem] * 3,
        scratch_shapes=scratch,
        compiler_params=pltpu.CompilerParams(vmem_limit_bytes=32 << 20),
        cost_estimate=pl.CostEstimate(flops=6 * rows * cols * nb, bytes_accessed=8 * rows * cols, transcendentals=0),
    )(piece, own, got, vh, vl, t, field, *prev)


def steps(eigvec, panels, factors):
    piece_t, block_t = tables()
    row, col = lax.axis_index("row"), lax.axis_index("col")
    piece = jnp.asarray(piece_t)[row]
    blocks = jnp.asarray(block_t)[row % 2, col]

    def over_x(v):
        u = send(v, X1)
        v = jnp.concatenate([v, u], axis=0)
        return v, send(v, X2)

    def over_z(v):
        return [v] + [send(v, ZL[d]) for d in (1, 2, 3)]

    first = over_z(panels[0])
    second = over_z(panels[1])
    hi, lo = prep(piece, eigvec)
    vs, ts, ws = [], [], []
    for k in range(NREF):
        if k < 2:
            a = jnp.concatenate([first, second][k], axis=0)
            parts, block = over_x(a), blocks[0]
        else:
            a = over_x(panels[2])
            a = jnp.concatenate(a, axis=0)
            parts, block = over_z(a), blocks[1]
        keep, give, vh, vl, *t = project(k, piece, block, parts, hi, lo, [u for pair in ts for u in pair])
        vs.append((vh, vl))
        if t:
            ts.append(t)
        w = send(give, CORE)
        w = keep + w
        h = w.shape[0] // 2
        u = send(w[h:], Y1)
        w = w[:h] + u
        u = send(w[h // 2:], Y2)
        w = w[:h // 2] + u
        u = send(w, ZH)
        w = w + u
        u = send(w, Y2)
        w = jnp.concatenate([w, u], axis=0)
        u = send(w, Y1)
        w = jnp.concatenate([w, u], axis=0)
        ws.append((w, send(w, CORE)))
    field = eigvec
    ss = []
    for k in range(NREF):
        field, *s = update(k, piece, *ws[k], *vs[k], factors[k], field, [u for pair in ss for u in pair])
        ss.append(s)
    return field


def solution(mesh):
    in_specs = (P("row", "col"), P(None, ("row", "col"), None), P())
    out_specs = P("row", "col")
    return jax.shard_map(steps, mesh=mesh, in_specs=in_specs, out_specs=out_specs, check_vma=False)
```

time: 154 us -> 151 us (0.981)
  the two profiles are of different devices: /device:TPU:33 before, /device:TPU:1 now
where the time goes in v1:
time: 151 us
  starting transfers between devices  57.5 us (38%)
  waiting for transfers between devices  53.8 us (36%)
  Pallas kernels  32.3 us (21%)
  local copies, waits for them, and re-layouts  5.95 us (4%)
    ppermute x36, starting transfers between devices, send(): return lax.ppermute(a, ('row', 'col'), perm)  57.5 us
    ppermute x36, waiting for transfers between devices, send(): return lax.ppermute(a, ('row', 'col'), perm)  53.8 us
    pallas_call x3, Pallas kernels, update(): pl.pallas_call(functools.partial(update_kernel, k, last), out_shape=[jax....  17.9 us
    pallas_call x3, Pallas kernels, project(): pl.pallas_call(functools.partial(project_kernel, k, last, len(parts)), ou...  11.1 us
    unnamed x15, local copies, waits for them, and re-layouts  3.42 us
    pallas_call x1, Pallas kernels, prep(): pl.pallas_call(prep_kernel, out_shape=[jax.ShapeDtypeStruct((cols, rows),...  3.31 us
  transfers between devices with their start and end apart: 36, of which 15 were waited for; matrix products, arithmetic and copies ran while one was open for 2% of the time, Pallas kernels for 17%

profile of v1, /device:TPU:1, one launch (start us, length us, event | category | flops | bytes accessed | tf_op | source)
XLA Modules:
  0.0 150.9 jit_solution(9823924069334721647)
XLA Ops:
  0.9 5.2 %collective-permute-start.12 = (f32[64,256]{1,0:T(8,128)S(1)}, f32[64,256]{1,0:T(8,128)S(1)}, u32[]{:S(2)}, u32[]{:S(2)}) collective-permute-start(f32[64,256]{1,0:T(8,128)S(1)} %get-tuple-element.56), channel_id=1, source_target_pairs={{0,3},{1,2},{2,1},{3,0},{4,7},{5,6},{6,5},{7,4},{8,11},{9,10},{10,... | collective-permute-start | bytes 196616 | tf_op jit(solution)/shard_map/ppermute | solution.py:46
  6.6 2.5 %collective-permute-start = (f32[64,256]{1,0:T(8,128)S(1)}, f32[64,256]{1,0:T(8,128)S(1)}, u32[]{:S(2)}, u32[]{:S(2)}) collective-permute-start(f32[64,256]{1,0:T(8,128)S(1)} %get-tuple-element.57), channel_id=1, source_target_pairs={{0,4},{1,5},{2,6},{3,7},{4,0},{5,1},{6,2},{7,3},{8,12},{9,13},{10,... | collective-permute-start | bytes 196616 | tf_op jit(solution)/shard_map/ppermute | solution.py:46
  9.0 3.2 %collective-permute-start.7 = (f32[64,256]{1,0:T(8,128)S(1)}, f32[64,256]{1,0:T(8,128)S(1)}, u32[]{:S(2)}, u32[]{:S(2)}) collective-permute-start(f32[64,256]{1,0:T(8,128)S(1)} %get-tuple-element.58), channel_id=1, source_target_pairs={{0,3},{1,2},{2,1},{3,0},{4,7},{5,6},{6,5},{7,4},{8,11},{9,10},{10,... | collective-permute-start | bytes 196616 | tf_op jit(solution)/shard_map/ppermute | solution.py:46
  13.8 2.5 %copy-done = f32[1024,1280]{1,0:T(8,128)S(1)} copy-done((f32[1024,1280]{1,0:T(8,128)S(1)}, f32[1024,1280]{1,0:T(8,128)}, u32[]{:S(2)}) %copy-start) | copy-done | bytes 5242904
  16.3 3.3 %prep.1 = (bf16[1280,1024]{1,0:T(8,128)(2,1)S(1)}, bf16[1280,1024]{1,0:T(8,128)(2,1)S(1)}) custom-call(s32[8]{0:T(128)S(1)} %dynamic-slice_bitcast_fusion.piece.refs_0_, f32[1024,1280]{1,0:T(8,128)S(1)} %copy-done), custom_call_target="tpu_custom_call" | custom-call | bytes 10485760 | tf_op jit(solution)/shard_map/prep/pallas_call | solution.py:97
  21.7 3.2 %collective-permute-done.6 = f32[64,256]{1,0:T(8,128)S(1)} collective-permute-done((f32[64,256]{1,0:T(8,128)S(1)}, f32[64,256]{1,0:T(8,128)S(1)}, u32[]{:S(2)}, u32[]{:S(2)}) %collective-permute-start.6) | collective-permute-done | bytes 65568 | tf_op jit(solution)/shard_map/ppermute | solution.py:46
  25.1 6.4 %collective-permute-done.8 = f32[256,256]{1,0:T(8,128)S(1)} collective-permute-done((f32[256,256]{1,0:T(8,128)S(1)}, f32[256,256]{1,0:T(8,128)S(1)}, u32[]{:S(2)}, u32[]{:S(2)}) %collective-permute-start.8) | collective-permute-done | bytes 262176 | tf_op jit(solution)/shard_map/ppermute | solution.py:46
  33.3 3.2 %collective-permute-start.4 = (f32[256,256]{1,0:T(8,128)S(1)}, f32[256,256]{1,0:T(8,128)S(1)}, u32[]{:S(2)}, u32[]{:S(2)}) collective-permute-start(f32[256,256]{1,0:T(8,128)S(1)} %pad_maximum_fusion.6.refs_2_), channel_id=1, source_target_pairs={{0,3},{1,2},{2,1},{3,0},{4,7},{5,6},{6,5},{7,4},{8,11},{9,10},{10,... | collective-permute-start | bytes 786440 | tf_op jit(solution)/shard_map/ppermute | solution.py:46
  36.9 3.1 %collective-permute-done.9.refs_3_ = f32[512,256]{1,0:T(8,128)S(1)} collective-permute-done((f32[512,256]{1,0:T(8,128)S(1)}, f32[512,256]{1,0:T(8,128)S(1)}, u32[]{:S(2)}, u32[]{:S(2)}) %collective-permute-start.9) | collective-permute-done | bytes 524320 | tf_op jit(solution)/shard_map/ppermute | solution.py:46
  40.0 3.9 %shard_map.55 = (f32[640,256]{1,0:T(8,128)S(1)}, f32[640,256]{1,0:T(8,128)S(1)}, bf16[1024,256]{1,0:T(8,128)(2,1)S(1)}, bf16[1024,256]{1,0:T(8,128)(2,1)S(1)}, b...) custom-call(s32[8]{0:T(128)S(1)} %dynamic-slice_bitcast_fusion.piece.refs_0_, ...), custom_call_target="tpu_custom_call" | custom-call | flops 2013265920 | bytes 7340032 | tf_op jit(solution)/shard_map/pallas_call | solution.py:178
  43.9 4.1 %collective-permute-start.29 = (f32[640,256]{1,0:T(8,128)S(1)}, f32[640,256]{1,0:T(8,128)S(1)}, u32[]{:S(2)}, u32[]{:S(2)}) collective-permute-start(f32[640,256]{1,0:T(8,128)S(1)} %get-tuple-element.44), channel_id=1, source_target_pairs={{0,16},{1,17},{2,18},{3,19},{4,20},{5,21},{6,22},{7,23},{8,24},{9,... | collective-permute-start | bytes 1966088 | tf_op jit(solution)/shard_map/ppermute | solution.py:46
  48.0 3.5 %shard_map.56 = (f32[768,256]{1,0:T(8,128)S(1)}, f32[768,256]{1,0:T(8,128)S(1)}, bf16[1024,256]{1,0:T(8,128)(2,1)S(1)}, bf16[1024,256]{1,0:T(8,128)(2,1)S(1)}, b...) custom-call(s32[8]{0:T(128)S(1)} %dynamic-slice_bitcast_fusion.piece.refs_0_, ...), custom_call_target="tpu_custom_call" | custom-call | flops 2415919104 | bytes 7340032 | tf_op jit(solution)/shard_map/pallas_call | solution.py:178
  53.0 5.2 %collective-permute-done.3.refs_4_ = f32[256,256]{1,0:T(8,128)S(1)} collective-permute-done((f32[256,256]{1,0:T(8,128)S(1)}, f32[256,256]{1,0:T(8,128)S(1)}, u32[]{:S(2)}, u32[]{:S(2)}) %collective-permute-start.3) | collective-permute-done | bytes 262176 | tf_op jit(solution)/shard_map/ppermute | solution.py:46
  58.3 3.7 %shard_map.57 = (f32[896,256]{1,0:T(8,128)S(1)}, f32[896,256]{1,0:T(8,128)S(1)}, bf16[1024,256]{1,0:T(8,128)(2,1)S(1)}, bf16[1024,256]{1,0:T(8,128)(2,1)S(1)}) custom-call(s32[8]{0:T(128)S(1)} %dynamic-slice_bitcast_fusion.piece.refs_0_, s32[16]{0:T(128)S(1)} %get-tuple-element.62.refs_1_, f32[256,256]{1,0:T(8,128)S(1)} %pad_maximum_fusion.6.refs_2_, ...), custom_call_target="tpu_custom_call" | custom-call | flops 2818572288 | bytes 7340032 | tf_op jit(solution)/shard_map/pallas_call | solution.py:178
  63.7 2.8 %collective-permute-start.30 = (f32[320,256]{1,0:T(8,128)S(1)}, f32[320,256]{1,0:T(8,128)S(1)}, u32[]{:S(2)}, u32[]{:S(2)}) collective-permute-start(f32[320,256]{1,0:T(8,128)S(1)} %slice.92), channel_id=1, source_target_pairs={{0,64},{1,65},{2,66},{3,67},{4,68},{5,69},{6,70},{7,71},{8,72},{9,... | collective-permute-start | bytes 983048 | tf_op jit(solution)/shard_map/ppermute | solution.py:46
  66.5 4.5 %collective-permute-done.30 = f32[320,256]{1,0:T(8,128)S(1)} collective-permute-done((f32[320,256]{1,0:T(8,128)S(1)}, f32[320,256]{1,0:T(8,128)S(1)}, u32[]{:S(2)}, u32[]{:S(2)}) %collective-permute-start.30) | collective-permute-done | bytes 327712 | tf_op jit(solution)/shard_map/ppermute | solution.py:46
  71.6 2.5 %collective-permute-start.23 = (f32[384,256]{1,0:T(8,128)S(1)}, f32[384,256]{1,0:T(8,128)S(1)}, u32[]{:S(2)}, u32[]{:S(2)}) collective-permute-start(f32[384,256]{1,0:T(8,128)S(1)} %slice.88), channel_id=1, source_target_pairs={{0,64},{1,65},{2,66},{3,67},{4,68},{5,69},{6,70},{7,71},{8,72},{9,... | collective-permute-start | bytes 1179656 | tf_op jit(solution)/shard_map/ppermute | solution.py:46
  75.7 4.9 %collective-permute-start.32 = (f32[160,256]{1,0:T(8,128)S(1)}, f32[160,256]{1,0:T(8,128)S(1)}, u32[]{:S(2)}, u32[]{:S(2)}) collective-permute-start(f32[160,256]{1,0:T(8,128)S(1)} %slice_add_fusion.5), channel_id=1, source_target_pairs={{0,32},{1,33},{2,34},{3,35},{4,36},{5,37},{6,38},{7,39},{8,40},{9,... | collective-permute-start | bytes 491528 | tf_op jit(solution)/shard_map/ppermute | solution.py:46
  81.6 4.4 %collective-permute-done.16 = f32[448,256]{1,0:T(8,128)S(1)} collective-permute-done((f32[448,256]{1,0:T(8,128)S(1)}, f32[448,256]{1,0:T(8,128)S(1)}, u32[]{:S(2)}, u32[]{:S(2)}) %collective-permute-start.16) | collective-permute-done | bytes 458784 | tf_op jit(solution)/shard_map/ppermute | solution.py:46
  86.6 1.6 %collective-permute-done.24 = f32[192,256]{1,0:T(8,128)S(1)} collective-permute-done((f32[192,256]{1,0:T(8,128)S(1)}, f32[192,256]{1,0:T(8,128)S(1)}, u32[]{:S(2)}, u32[]{:S(2)}) %collective-permute-start.24) | collective-permute-done | bytes 196640 | tf_op jit(solution)/shard_map/ppermute | solution.py:46
  88.2 4.9 %collective-permute-start.25 = (f32[192,256]{1,0:T(8,128)S(1)}, f32[192,256]{1,0:T(8,128)S(1)}, u32[]{:S(2)}, u32[]{:S(2)}) collective-permute-start(f32[192,256]{1,0:T(8,128)S(1)} %slice_add_fusion.4), channel_id=1, source_target_pairs={{0,32},{1,33},{2,34},{3,35},{4,36},{5,37},{6,38},{7,39},{8,40},{9,... | collective-permute-start | bytes 589832 | tf_op jit(solution)/shard_map/ppermute | solution.py:46
  93.1 3.6 %collective-permute-start.18 = (f32[224,256]{1,0:T(8,128)S(1)}, f32[224,256]{1,0:T(8,128)S(1)}, u32[]{:S(2)}, u32[]{:S(2)}) collective-permute-start(f32[224,256]{1,0:T(8,128)S(1)} %slice_add_fusion.3), channel_id=1, source_target_pairs={{0,32},{1,33},{2,34},{3,35},{4,36},{5,37},{6,38},{7,39},{8,40},{9,... | collective-permute-start | bytes 688136 | tf_op jit(solution)/shard_map/ppermute | solution.py:46
  97.9 2.4 %collective-permute-done.25 = f32[192,256]{1,0:T(8,128)S(1)} collective-permute-done((f32[192,256]{1,0:T(8,128)S(1)}, f32[192,256]{1,0:T(8,128)S(1)}, u32[]{:S(2)}, u32[]{:S(2)}) %collective-permute-start.25) | collective-permute-done | bytes 196640 | tf_op jit(solution)/shard_map/ppermute | solution.py:46
  101.4 10.0 %collective-permute-done.18 = f32[224,256]{1,0:T(8,128)S(1)} collective-permute-done((f32[224,256]{1,0:T(8,128)S(1)}, f32[224,256]{1,0:T(8,128)S(1)}, u32[]{:S(2)}, u32[]{:S(2)}) %collective-permute-start.18) | collective-permute-done | bytes 229408 | tf_op jit(solution)/shard_map/ppermute | solution.py:46
  112.1 3.6 %collective-permute-start.34 = (f32[320,256]{1,0:T(8,128)S(1)}, f32[320,256]{1,0:T(8,128)S(1)}, u32[]{:S(2)}, u32[]{:S(2)}) collective-permute-start(f32[320,256]{1,0:T(8,128)S(1)} %pad_maximum_fusion.5), channel_id=1, source_target_pairs={{0,64},{1,65},{2,66},{3,67},{4,68},{5,69},{6,70},{7,71},{8,72},{9,... | collective-permute-start | bytes 983048 | tf_op jit(solution)/shard_map/ppermute | solution.py:46
  116.5 2.8 %collective-permute-start.20 = (f32[448,256]{1,0:T(8,128)S(1)}, f32[448,256]{1,0:T(8,128)S(1)}, u32[]{:S(2)}, u32[]{:S(2)}) collective-permute-start(f32[448,256]{1,0:T(8,128)S(1)} %pad_maximum_fusion.3), channel_id=1, source_target_pairs={{0,64},{1,65},{2,66},{3,67},{4,68},{5,69},{6,70},{7,71},{8,72},{9,... | collective-permute-start | bytes 1376264 | tf_op jit(solution)/shard_map/ppermute | solution.py:46
  119.3 3.5 %collective-permute-done.34 = f32[320,256]{1,0:T(8,128)S(1)} collective-permute-done((f32[320,256]{1,0:T(8,128)S(1)}, f32[320,256]{1,0:T(8,128)S(1)}, u32[]{:S(2)}, u32[]{:S(2)}) %collective-permute-start.34) | collective-permute-done | bytes 327712 | tf_op jit(solution)/shard_map/ppermute | solution.py:46
  123.8 3.1 %collective-permute-done.27 = f32[384,256]{1,0:T(8,128)S(1)} collective-permute-done((f32[384,256]{1,0:T(8,128)S(1)}, f32[384,256]{1,0:T(8,128)S(1)}, u32[]{:S(2)}, u32[]{:S(2)}) %collective-permute-start.27) | collective-permute-done | bytes 393248 | tf_op jit(solution)/shard_map/ppermute | solution.py:46
  127.6 4.2 %collective-permute-done.20 = f32[448,256]{1,0:T(8,128)S(1)} collective-permute-done((f32[448,256]{1,0:T(8,128)S(1)}, f32[448,256]{1,0:T(8,128)S(1)}, u32[]{:S(2)}, u32[]{:S(2)}) %collective-permute-start.20) | collective-permute-done | bytes 458784 | tf_op jit(solution)/shard_map/ppermute | solution.py:46
  132.8 5.9 %shard_map.58 = (f32[1024,1280]{1,0:T(8,128)S(1)}, bf16[1280,256]{1,0:T(8,128)(2,1)S(1)}, bf16[1280,256]{1,0:T(8,128)(2,1)S(1)}) custom-call(s32[8]{0:T(128)S(1)} %dynamic-slice_bitcast_fusion.piece.refs_0_, f32[640,256]{1,0:T(8,128)S(1)} %pad_maximum_fusion.2.refs_1_, f32[640,256]{1,0:T(8,128)S(1)} %collective-permute-done.35.refs_2_, ...), custom_call_target="tpu_custom_call" | custom-call | flops 2013265920 | bytes 10485760 | tf_op jit(solution)/shard_map/pallas_call | solution.py:268
  138.7 5.1 %shard_map.59 = (f32[1024,1280]{1,0:T(8,128)S(1)}, bf16[1280,256]{1,0:T(8,128)(2,1)S(1)}, bf16[1280,256]{1,0:T(8,128)(2,1)S(1)}) custom-call(s32[8]{0:T(128)S(1)} %dynamic-slice_bitcast_fusion.piece.refs_0_, f32[768,256]{1,0:T(8,128)S(1)} %pad_maximum_fusion.1.refs_1_, f32[768,256]{1,0:T(8,128)S(1)} %collective-permute-done.28.refs_2_, ...), custom_call_target="tpu_custom_call" | custom-call | flops 2013265920 | bytes 10485760 | tf_op jit(solution)/shard_map/pallas_call | solution.py:268
  143.8 6.9 %shard_map.60 = f32[1024,1280]{1,0:T(8,128)} custom-call(s32[8]{0:T(128)S(1)} %dynamic-slice_bitcast_fusion.piece.refs_0_, f32[896,256]{1,0:T(8,128)S(1)} %pad_maximum_fusion.refs_1_, f32[896,256]{1,0:T(8,128)S(1)} %collective-permute-done.21.refs_2_, bf16[1024,256]{1,0:T(8,128)(2,1)S(1)} %get-tuple-element.37.refs_3_, ...), custom_call_target="tpu_custom_call" | custom-call | flops 2013265920 | bytes 10485760 | tf_op jit(solution)/shard_map/pallas_call | solution.py:268
  (98 shorter events, 20.8 us)
Async XLA Ops:
  0.9 19.4 %collective-permute-start.12 = (f32[64,256]{1,0:T(8,128)S(1)}, f32[64,256]{1,0:T(8,128)S(1)}, u32[]{:S(2)}, u32[]{:S(2)}) collective-permute-start(f32[64,256]{1,0:T(8,128)S(1)} %get-tuple-element.56), channel_id=1, source_target_pairs={{0,3},{1,2},{2,1},{3,0},{4,7},{5,6},{6,5},{7,4},{8,11},{9,10},{10,... | collective-permute-start | bytes 196616 | tf_op jit(solution)/shard_map/ppermute | solution.py:46
  6.2 14.6 %collective-permute-start.11 = (f32[64,256]{1,0:T(8,128)S(1)}, f32[64,256]{1,0:T(8,128)S(1)}, u32[]{:S(2)}, u32[]{:S(2)}) collective-permute-start(f32[64,256]{1,0:T(8,128)S(1)} %get-tuple-element.56), channel_id=1, source_target_pairs={{0,2},{1,3},{2,0},{3,1},{4,6},{5,7},{6,4},{7,5},{8,10},{9,11},{10,... | collective-permute-start | bytes 196616 | tf_op jit(solution)/shard_map/ppermute | solution.py:46
  6.2 14.6 %collective-permute-start.10 = (f32[64,256]{1,0:T(8,128)S(1)}, f32[64,256]{1,0:T(8,128)S(1)}, u32[]{:S(2)}, u32[]{:S(2)}) collective-permute-start(f32[64,256]{1,0:T(8,128)S(1)} %get-tuple-element.56), channel_id=1, source_target_pairs={{0,1},{1,0},{2,3},{3,2},{4,5},{5,4},{6,7},{7,6},{8,9},{9,8},{10,11... | collective-permute-start | bytes 196616 | tf_op jit(solution)/shard_map/ppermute | solution.py:46
  6.6 13.7 %collective-permute-start = (f32[64,256]{1,0:T(8,128)S(1)}, f32[64,256]{1,0:T(8,128)S(1)}, u32[]{:S(2)}, u32[]{:S(2)}) collective-permute-start(f32[64,256]{1,0:T(8,128)S(1)} %get-tuple-element.57), channel_id=1, source_target_pairs={{0,4},{1,5},{2,6},{3,7},{4,0},{5,1},{6,2},{7,3},{8,12},{9,13},{10,... | collective-permute-start | bytes 196616 | tf_op jit(solution)/shard_map/ppermute | solution.py:46
  9.0 12.7 %collective-permute-start.7 = (f32[64,256]{1,0:T(8,128)S(1)}, f32[64,256]{1,0:T(8,128)S(1)}, u32[]{:S(2)}, u32[]{:S(2)}) collective-permute-start(f32[64,256]{1,0:T(8,128)S(1)} %get-tuple-element.58), channel_id=1, source_target_pairs={{0,3},{1,2},{2,1},{3,0},{4,7},{5,6},{6,5},{7,4},{8,11},{9,10},{10,... | collective-permute-start | bytes 196616 | tf_op jit(solution)/shard_map/ppermute | solution.py:46
  20.8 12.5 %collective-permute-start.1 = (f32[128,256]{1,0:T(8,128)S(1)}, f32[128,256]{1,0:T(8,128)S(1)}, u32[]{:S(2)}, u32[]{:S(2)}) collective-permute-start(f32[128,256]{1,0:T(8,128)S(1)} %pad_maximum_fusion.9), channel_id=1, source_target_pairs={{0,12},{1,13},{2,14},{3,15},{4,8},{5,9},{6,10},{7,11},{8,4},{9,5},... | collective-permute-start | bytes 393224 | tf_op jit(solution)/shard_map/ppermute | solution.py:46
  20.8 11.4 %collective-permute-start.13 = (f32[256,256]{1,0:T(8,128)S(1)}, f32[256,256]{1,0:T(8,128)S(1)}, u32[]{:S(2)}, u32[]{:S(2)}) collective-permute-start(f32[256,256]{1,0:T(8,128)S(1)} %pad_maximum_fusion.8), channel_id=1, source_target_pairs={{0,4},{1,5},{2,6},{3,7},{4,0},{5,1},{6,2},{7,3},{8,12},{9,13},{10,... | collective-permute-start | bytes 786440 | tf_op jit(solution)/shard_map/ppermute | solution.py:46
  24.9 6.6 %collective-permute-start.8 = (f32[256,256]{1,0:T(8,128)S(1)}, f32[256,256]{1,0:T(8,128)S(1)}, u32[]{:S(2)}, u32[]{:S(2)}) collective-permute-start(f32[256,256]{1,0:T(8,128)S(1)} %pad_maximum_fusion.7), channel_id=1, source_target_pairs={{0,4},{1,5},{2,6},{3,7},{4,0},{5,1},{6,2},{7,3},{8,12},{9,13},{10,... | collective-permute-start | bytes 786440 | tf_op jit(solution)/shard_map/ppermute | solution.py:46
  31.6 8.4 %collective-permute-start.9 = (f32[512,256]{1,0:T(8,128)S(1)}, f32[512,256]{1,0:T(8,128)S(1)}, u32[]{:S(2)}, u32[]{:S(2)}) collective-permute-start(f32[512,256]{1,0:T(8,128)S(1)} %constant_dynamic-update-slice_fusion.refs_2_), channel_id=1, source_target_pairs={{0,12},{1,13},{2,14},{3,15},{4,8},{5,9},{6,10},{7,11},{8,4},{9,5},... | collective-permute-start | bytes 1572872 | tf_op jit(solution)/shard_map/ppermute | solution.py:46
  32.2 15.7 %collective-permute-start.14 = (f32[512,256]{1,0:T(8,128)S(1)}, f32[512,256]{1,0:T(8,128)S(1)}, u32[]{:S(2)}, u32[]{:S(2)}) collective-permute-start(f32[512,256]{1,0:T(8,128)S(1)} %constant_dynamic-update-slice_fusion.5.refs_2_), channel_id=1, source_target_pairs={{0,12},{1,13},{2,14},{3,15},{4,8},{5,9},{6,10},{7,11},{8,4},{9,5},... | collective-permute-start | bytes 1572872 | tf_op jit(solution)/shard_map/ppermute | solution.py:46
  33.3 19.7 %collective-permute-start.4 = (f32[256,256]{1,0:T(8,128)S(1)}, f32[256,256]{1,0:T(8,128)S(1)}, u32[]{:S(2)}, u32[]{:S(2)}) collective-permute-start(f32[256,256]{1,0:T(8,128)S(1)} %pad_maximum_fusion.6.refs_2_), channel_id=1, source_target_pairs={{0,3},{1,2},{2,1},{3,0},{4,7},{5,6},{6,5},{7,4},{8,11},{9,10},{10,... | collective-permute-start | bytes 786440 | tf_op jit(solution)/shard_map/ppermute | solution.py:46
  36.5 21.7 %collective-permute-start.3 = (f32[256,256]{1,0:T(8,128)S(1)}, f32[256,256]{1,0:T(8,128)S(1)}, u32[]{:S(2)}, u32[]{:S(2)}) collective-permute-start(f32[256,256]{1,0:T(8,128)S(1)} %pad_maximum_fusion.6.refs_2_), channel_id=1, source_target_pairs={{0,2},{1,3},{2,0},{3,1},{4,6},{5,7},{6,4},{7,5},{8,10},{9,11},{10,... | collective-permute-start | bytes 786440 | tf_op jit(solution)/shard_map/ppermute | solution.py:46
  36.5 21.7 %collective-permute-start.2 = (f32[256,256]{1,0:T(8,128)S(1)}, f32[256,256]{1,0:T(8,128)S(1)}, u32[]{:S(2)}, u32[]{:S(2)}) collective-permute-start(f32[256,256]{1,0:T(8,128)S(1)} %pad_maximum_fusion.6.refs_2_), channel_id=1, source_target_pairs={{0,1},{1,0},{2,3},{3,2},{4,5},{5,4},{6,7},{7,6},{8,9},{9,8},{10,11... | collective-permute-start | bytes 786440 | tf_op jit(solution)/shard_map/ppermute | solution.py:46
  43.9 19.7 %collective-permute-start.29 = (f32[640,256]{1,0:T(8,128)S(1)}, f32[640,256]{1,0:T(8,128)S(1)}, u32[]{:S(2)}, u32[]{:S(2)}) collective-permute-start(f32[640,256]{1,0:T(8,128)S(1)} %get-tuple-element.44), channel_id=1, source_target_pairs={{0,16},{1,17},{2,18},{3,19},{4,20},{5,21},{6,22},{7,23},{8,24},{9,... | collective-permute-start | bytes 1966088 | tf_op jit(solution)/shard_map/ppermute | solution.py:46
  51.4 20.0 %collective-permute-start.22 = (f32[768,256]{1,0:T(8,128)S(1)}, f32[768,256]{1,0:T(8,128)S(1)}, u32[]{:S(2)}, u32[]{:S(2)}) collective-permute-start(f32[768,256]{1,0:T(8,128)S(1)} %get-tuple-element.40), channel_id=1, source_target_pairs={{0,16},{1,17},{2,18},{3,19},{4,20},{5,21},{6,22},{7,23},{8,24},{9,... | collective-permute-start | bytes 2359304 | tf_op jit(solution)/shard_map/ppermute | solution.py:46
  62.0 12.1 %collective-permute-start.15 = (f32[896,256]{1,0:T(8,128)S(1)}, f32[896,256]{1,0:T(8,128)S(1)}, u32[]{:S(2)}, u32[]{:S(2)}) collective-permute-start(f32[896,256]{1,0:T(8,128)S(1)} %get-tuple-element.36), channel_id=1, source_target_pairs={{0,16},{1,17},{2,18},{3,19},{4,20},{5,21},{6,22},{7,23},{8,24},{9,... | collective-permute-start | bytes 2752520 | tf_op jit(solution)/shard_map/ppermute | solution.py:46
  63.7 7.3 %collective-permute-start.30 = (f32[320,256]{1,0:T(8,128)S(1)}, f32[320,256]{1,0:T(8,128)S(1)}, u32[]{:S(2)}, u32[]{:S(2)}) collective-permute-start(f32[320,256]{1,0:T(8,128)S(1)} %slice.92), channel_id=1, source_target_pairs={{0,64},{1,65},{2,66},{3,67},{4,68},{5,69},{6,70},{7,71},{8,72},{9,... | collective-permute-start | bytes 983048 | tf_op jit(solution)/shard_map/ppermute | solution.py:46
  71.6 9.5 %collective-permute-start.23 = (f32[384,256]{1,0:T(8,128)S(1)}, f32[384,256]{1,0:T(8,128)S(1)}, u32[]{:S(2)}, u32[]{:S(2)}) collective-permute-start(f32[384,256]{1,0:T(8,128)S(1)} %slice.88), channel_id=1, source_target_pairs={{0,64},{1,65},{2,66},{3,67},{4,68},{5,69},{6,70},{7,71},{8,72},{9,... | collective-permute-start | bytes 1179656 | tf_op jit(solution)/shard_map/ppermute | solution.py:46
  74.3 11.8 %collective-permute-start.16 = (f32[448,256]{1,0:T(8,128)S(1)}, f32[448,256]{1,0:T(8,128)S(1)}, u32[]{:S(2)}, u32[]{:S(2)}) collective-permute-start(f32[448,256]{1,0:T(8,128)S(1)} %slice.84), channel_id=1, source_target_pairs={{0,64},{1,65},{2,66},{3,67},{4,68},{5,69},{6,70},{7,71},{8,72},{9,... | collective-permute-start | bytes 1376264 | tf_op jit(solution)/shard_map/ppermute | solution.py:46
  75.7 21.0 %collective-permute-start.32 = (f32[160,256]{1,0:T(8,128)S(1)}, f32[160,256]{1,0:T(8,128)S(1)}, u32[]{:S(2)}, u32[]{:S(2)}) collective-permute-start(f32[160,256]{1,0:T(8,128)S(1)} %slice_add_fusion.5), channel_id=1, source_target_pairs={{0,32},{1,33},{2,34},{3,35},{4,36},{5,37},{6,38},{7,39},{8,40},{9,... | collective-permute-start | bytes 491528 | tf_op jit(solution)/shard_map/ppermute | solution.py:46
  81.2 7.0 %collective-permute-start.24 = (f32[192,256]{1,0:T(8,128)S(1)}, f32[192,256]{1,0:T(8,128)S(1)}, u32[]{:S(2)}, u32[]{:S(2)}) collective-permute-start(f32[192,256]{1,0:T(8,128)S(1)} %slice.90), channel_id=1, source_target_pairs={{0,192},{1,193},{2,194},{3,195},{4,196},{5,197},{6,198},{7,199},{8... | collective-permute-start | bytes 589832 | tf_op jit(solution)/shard_map/ppermute | solution.py:46
  86.1 7.0 %collective-permute-start.17 = (f32[224,256]{1,0:T(8,128)S(1)}, f32[224,256]{1,0:T(8,128)S(1)}, u32[]{:S(2)}, u32[]{:S(2)}) collective-permute-start(f32[224,256]{1,0:T(8,128)S(1)} %slice.86), channel_id=1, source_target_pairs={{0,192},{1,193},{2,194},{3,195},{4,196},{5,197},{6,198},{7,199},{8... | collective-permute-start | bytes 688136 | tf_op jit(solution)/shard_map/ppermute | solution.py:46
  88.2 12.1 %collective-permute-start.25 = (f32[192,256]{1,0:T(8,128)S(1)}, f32[192,256]{1,0:T(8,128)S(1)}, u32[]{:S(2)}, u32[]{:S(2)}) collective-permute-start(f32[192,256]{1,0:T(8,128)S(1)} %slice_add_fusion.4), channel_id=1, source_target_pairs={{0,32},{1,33},{2,34},{3,35},{4,36},{5,37},{6,38},{7,39},{8,40},{9,... | collective-permute-start | bytes 589832 | tf_op jit(solution)/shard_map/ppermute | solution.py:46
  93.1 18.4 %collective-permute-start.18 = (f32[224,256]{1,0:T(8,128)S(1)}, f32[224,256]{1,0:T(8,128)S(1)}, u32[]{:S(2)}, u32[]{:S(2)}) collective-permute-start(f32[224,256]{1,0:T(8,128)S(1)} %slice_add_fusion.3), channel_id=1, source_target_pairs={{0,32},{1,33},{2,34},{3,35},{4,36},{5,37},{6,38},{7,39},{8,40},{9,... | collective-permute-start | bytes 688136 | tf_op jit(solution)/shard_map/ppermute | solution.py:46
  96.7 15.3 %collective-permute-start.33 = (f32[160,256]{1,0:T(8,128)S(1)}, f32[160,256]{1,0:T(8,128)S(1)}, u32[]{:S(2)}, u32[]{:S(2)}) collective-permute-start(f32[160,256]{1,0:T(8,128)S(1)} %add.64), channel_id=1, source_target_pairs={{0,192},{1,193},{2,194},{3,195},{4,196},{5,197},{6,198},{7,199},{8... | collective-permute-start | bytes 491528 | tf_op jit(solution)/shard_map/ppermute | solution.py:46
  100.3 15.4 %collective-permute-start.26 = (f32[192,256]{1,0:T(8,128)S(1)}, f32[192,256]{1,0:T(8,128)S(1)}, u32[]{:S(2)}, u32[]{:S(2)}) collective-permute-start(f32[192,256]{1,0:T(8,128)S(1)} %add.60), channel_id=1, source_target_pairs={{0,192},{1,193},{2,194},{3,195},{4,196},{5,197},{6,198},{7,199},{8... | collective-permute-start | bytes 589832 | tf_op jit(solution)/shard_map/ppermute | solution.py:46
  112.1 10.7 %collective-permute-start.34 = (f32[320,256]{1,0:T(8,128)S(1)}, f32[320,256]{1,0:T(8,128)S(1)}, u32[]{:S(2)}, u32[]{:S(2)}) collective-permute-start(f32[320,256]{1,0:T(8,128)S(1)} %pad_maximum_fusion.5), channel_id=1, source_target_pairs={{0,64},{1,65},{2,66},{3,67},{4,68},{5,69},{6,70},{7,71},{8,72},{9,... | collective-permute-start | bytes 983048 | tf_op jit(solution)/shard_map/ppermute | solution.py:46
  115.8 11.1 %collective-permute-start.27 = (f32[384,256]{1,0:T(8,128)S(1)}, f32[384,256]{1,0:T(8,128)S(1)}, u32[]{:S(2)}, u32[]{:S(2)}) collective-permute-start(f32[384,256]{1,0:T(8,128)S(1)} %pad_maximum_fusion.4), channel_id=1, source_target_pairs={{0,64},{1,65},{2,66},{3,67},{4,68},{5,69},{6,70},{7,71},{8,72},{9,... | collective-permute-start | bytes 1179656 | tf_op jit(solution)/shard_map/ppermute | solution.py:46
  116.5 15.3 %collective-permute-start.20 = (f32[448,256]{1,0:T(8,128)S(1)}, f32[448,256]{1,0:T(8,128)S(1)}, u32[]{:S(2)}, u32[]{:S(2)}) collective-permute-start(f32[448,256]{1,0:T(8,128)S(1)} %pad_maximum_fusion.3), channel_id=1, source_target_pairs={{0,64},{1,65},{2,66},{3,67},{4,68},{5,69},{6,70},{7,71},{8,72},{9,... | collective-permute-start | bytes 1376264 | tf_op jit(solution)/shard_map/ppermute | solution.py:46
  122.8 10.0 %collective-permute-start.35 = (f32[640,256]{1,0:T(8,128)S(1)}, f32[640,256]{1,0:T(8,128)S(1)}, u32[]{:S(2)}, u32[]{:S(2)}) collective-permute-start(f32[640,256]{1,0:T(8,128)S(1)} %pad_maximum_fusion.2.refs_1_), channel_id=1, source_target_pairs={{0,16},{1,17},{2,18},{3,19},{4,20},{5,21},{6,22},{7,23},{8,24},{9,... | collective-permute-start | bytes 1966088 | tf_op jit(solution)/shard_map/ppermute | solution.py:46
  126.9 11.8 %collective-permute-start.28 = (f32[768,256]{1,0:T(8,128)S(1)}, f32[768,256]{1,0:T(8,128)S(1)}, u32[]{:S(2)}, u32[]{:S(2)}) collective-permute-start(f32[768,256]{1,0:T(8,128)S(1)} %pad_maximum_fusion.1.refs_1_), channel_id=1, source_target_pairs={{0,16},{1,17},{2,18},{3,19},{4,20},{5,21},{6,22},{7,23},{8,24},{9,... | collective-permute-start | bytes 2359304 | tf_op jit(solution)/shard_map/ppermute | solution.py:46
  131.8 12.0 %collective-permute-start.21 = (f32[896,256]{1,0:T(8,128)S(1)}, f32[896,256]{1,0:T(8,128)S(1)}, u32[]{:S(2)}, u32[]{:S(2)}) collective-permute-start(f32[896,256]{1,0:T(8,128)S(1)} %pad_maximum_fusion.refs_1_), channel_id=1, source_target_pairs={{0,16},{1,17},{2,18},{3,19},{4,20},{5,21},{6,22},{7,23},{8,24},{9,... | collective-permute-start | bytes 2752520 | tf_op jit(solution)/shard_map/ppermute | solution.py:46
  (8 other events, 140.4 us)
